TPU v7x, 512 devices: a whole 4x8x8 slice. The times are simulated.
512 devices in a mesh: tm: 16 (over y, core), row: 8 (over z), col: 4 (over x).
Axes of the slice: x: 4, y: 8, z: 8, core: 2. Of those that a mesh axis runs over, the one named last changes fastest.
Arguments:
- frames: bfloat16 [256, 2, 128, 512], P('tm', None, 'row', 'col'), may hold values from -6 to 6
- phase: int32 [256], P('tm'), may hold values from 0 to 15
- shift: int32 [2, 8, 32], P(None, 'row', 'col'), may hold values from -6 to 6
- interp_rows: bfloat16 [32, 36], replicated, may hold values from -0.75 to 1.75, as said below
- interp_cols: bfloat16 [32, 36], replicated, may hold values from -0.75 to 1.75, as said below
Outputs:
- ensemble: float32 [16, 8, 32, 1024], P('tm', 'row', 'col')
Inputs may be any that keep to these rules, and one draw needn't show every extreme that they name: `interp_rows`: row i is zero outside columns i to i + 4. `interp_cols`: row i is zero outside columns i to i + 4.
All inputs are finite; a program needn't handle non-finite values.
Results may differ from a plain program's by a relative error of at most 0.0077.
Values may be sent and summed in bfloat16 or wider, within the bound.
No kernel may reach another device: no remote copies, remote signals or barrier semaphores. Data moves between devices by JAX's collectives and lax.ppermute only.
A program may use at most 64 MiB of HBM per device.

v0:
```python
from functools import partial
import math

import jax
import jax.numpy as jnp
from jax import lax
from jax.sharding import PartitionSpec as P

WIN = 32
STEP = 16
BAND = 2
BIN_DEV = 1
HALO = 16


HIGHEST_PRECISION = lax.Precision.HIGHEST


def with_halo(cells, sides, width):
    for axis, dim in sides:
        count = lax.axis_size(axis)
        ends = count - 1
        head = lax.slice_in_dim(cells, 0, width, axis=dim)
        tail = lax.slice_in_dim(cells, cells.shape[dim] - width, cells.shape[dim], axis=dim)
        cells = jnp.concatenate(
            [
                lax.ppermute(tail, axis, [(i, (i + 1) % count) for i in range(ends)]),
                cells,
                lax.ppermute(head, axis, [((i + 1) % count, i) for i in range(ends)]),
            ],
            axis=dim,
        )
    return cells


def window_cut(picture, row_start, col_start, extent):
    return lax.dynamic_slice(picture, (row_start, col_start), (extent, extent))


def cut_windows(picture, row_starts, col_starts, extent):
    return jax.vmap(partial(window_cut, extent=extent), in_axes=(None, 0, 0))(
        picture, row_starts, col_starts
    )


def angle_tables():
    indices = jnp.arange(WIN, dtype=jnp.int32)
    product = indices[:, None] * indices[None, :] % WIN
    angles = product.astype(jnp.float32) * (2.0 * math.pi / WIN)
    return (jnp.cos(angles), jnp.sin(angles))


def forward(centred, cosine_half, sine_half):
    right_table = jnp.concatenate([cosine_half, -sine_half], axis=1)
    halved = jnp.einsum(
        "abn,bk->akn", centred, right_table, preferred_element_type=jnp.float32
    ).astype(jnp.bfloat16)
    left_table = jnp.concatenate([cosine_half, sine_half], axis=0)
    stacked = jnp.einsum("ja,akn->jkn", left_table, halved, preferred_element_type=jnp.float32)
    real_part = stacked[:WIN, :WIN] + stacked[WIN:, WIN:]
    imag_part = stacked[:WIN, WIN:] - stacked[WIN:, :WIN]
    return (real_part, imag_part)


def inverse(real_part, imag_part, cosine_full, sine_full):
    section_real = jnp.einsum(
        "jkn,kv->jvn", real_part, cosine_full, precision=HIGHEST_PRECISION
    ) - jnp.einsum("jkn,kv->jvn", imag_part, sine_full, precision=HIGHEST_PRECISION)
    section_imag = jnp.einsum(
        "jkn,kv->jvn", real_part, sine_full, precision=HIGHEST_PRECISION
    ) + jnp.einsum("jkn,kv->jvn", imag_part, cosine_full, precision=HIGHEST_PRECISION)
    planes = jnp.einsum(
        "uj,jvn->uvn", cosine_full, section_real, precision=HIGHEST_PRECISION
    ) - jnp.einsum("uj,jvn->uvn", sine_full, section_imag, precision=HIGHEST_PRECISION)
    return planes * (1.0 / WIN**3)


def centre_window(values):
    return (values - jnp.mean(values, axis=(0, 1), keepdims=True)).astype(jnp.bfloat16)


def body(frames, phase, shift, interp_rows, interp_cols):
    pairs_dev = frames.shape[0]
    tile_rows = frames.shape[2]
    tile_cols = frames.shape[3]
    extended = with_halo(frames, (("row", 2), ("col", 3)), HALO)
    win_rows = tile_rows // STEP
    win_cols = tile_cols // STEP
    win_count = win_rows * win_cols
    indices = jnp.arange(win_count, dtype=jnp.int32)
    base_start = HALO - (WIN - STEP) // 2
    start_rows = base_start + STEP * (indices // win_cols)
    start_cols = base_start + STEP * (indices % win_cols)
    patch_rows = start_rows + shift[0].reshape(-1) - BAND
    patch_cols = start_cols + shift[1].reshape(-1) - BAND
    group_size = math.gcd(pairs_dev, 8)
    turn_count = pairs_dev // group_size
    blocks = extended.reshape(turn_count, group_size, 2, extended.shape[2], extended.shape[3])
    phases = phase.reshape(turn_count, group_size)
    bin_total = BIN_DEV * lax.axis_size("tm")
    bin_ids = jnp.arange(bin_total, dtype=jnp.int32)
    cosine_full, sine_full = angle_tables()
    cosine_half = cosine_full.astype(jnp.bfloat16)
    sine_half = sine_full.astype(jnp.bfloat16)
    cut_first = partial(cut_windows, row_starts=start_rows, col_starts=start_cols, extent=WIN)
    cut_second = partial(
        cut_windows, row_starts=patch_rows, col_starts=patch_cols, extent=WIN + 2 * BAND
    )

    def cross_of(pair_block):
        wins_a = jax.vmap(cut_first)(pair_block[:, 0])
        patches = jax.vmap(cut_second)(pair_block[:, 1])
        lifted = jnp.einsum(
            "ia,gwab->gwib", interp_rows, patches, preferred_element_type=jnp.float32
        ).astype(jnp.bfloat16)
        deformed = jnp.einsum(
            "gwib,jb->ijgw", lifted, interp_cols, preferred_element_type=jnp.float32
        )
        centred_b = centre_window(deformed).reshape(WIN, WIN, group_size * win_count)
        centred_a = centre_window(jnp.transpose(wins_a, (2, 3, 0, 1)).astype(jnp.float32)).reshape(
            WIN, WIN, group_size * win_count
        )
        a_real, a_imag = forward(centred_a, cosine_half, sine_half)
        b_real, b_imag = forward(centred_b, cosine_half, sine_half)
        cross_real = a_real * b_real + a_imag * b_imag
        cross_imag = a_real * b_imag - a_imag * b_real
        return (cross_real, cross_imag)

    def bin_onehot(phase_block):
        return (phase_block[None, :] == bin_ids[:, None]).astype(jnp.float32)

    def spectrum_step(running, inputs):
        pair_block, phase_block = inputs
        cross_real, cross_imag = cross_of(pair_block)
        onehot_bins = bin_onehot(phase_block)
        real_add = jnp.einsum(
            "bg,jkgw->jkbw",
            onehot_bins,
            cross_real.reshape(WIN, WIN, group_size, win_count),
            precision=HIGHEST_PRECISION,
        )
        imag_add = jnp.einsum(
            "bg,jkgw->jkbw",
            onehot_bins,
            cross_imag.reshape(WIN, WIN, group_size, win_count),
            precision=HIGHEST_PRECISION,
        )
        return ((running[0] + real_add, running[1] + imag_add), None)

    initial = jnp.zeros((WIN, WIN, bin_total, win_count), jnp.float32)
    totals, _ = lax.scan(spectrum_step, (initial, initial), (blocks, phases))
    real_own, imag_own = (
        lax.psum_scatter(totals[0], "tm", scatter_dimension=2, tiled=True),
        lax.psum_scatter(totals[1], "tm", scatter_dimension=2, tiled=True),
    )
    planes = inverse(
        real_own.reshape(WIN, WIN, BIN_DEV * win_count),
        imag_own.reshape(WIN, WIN, BIN_DEV * win_count),
        cosine_full,
        sine_full,
    )
    planes = planes.reshape(WIN, WIN, BIN_DEV, win_rows, win_cols)
    result = jnp.transpose(planes, (2, 3, 4, 0, 1)).reshape(BIN_DEV, win_rows, win_cols, WIN * WIN)
    return result


def solution(mesh):
    placed = (P("tm", None, "row", "col"), P("tm"), P(None, "row", "col"), P(), P())
    return jax.shard_map(
        body, mesh=mesh, in_specs=placed, out_specs=P("tm", "row", "col", None), check_vma=False
    )
```

profile of v0, /device:TPU:27, one launch (start us, length us, event | category | flops | bytes accessed | tf_op | source)
XLA Modules:
  0.0 276.5 jit_solution(888998667544686159)
XLA Ops:
  6.5 4.1 %collective-permute-start = (bf16[16,2,16,128]{3,2,1,0:T(8,128)(2,1)}, bf16[16,2,16,128]{3,2,1,0:T(8,128)(2,1)S(1)}, u32[]{:S(2)}, u32[]{:S(2)}) collective-permute-start(bf16[16,2,16,128]{3,2,1,0:T(8,128)(2,1)} %param.7), channel_id=1, source_target_pairs={{0,4},{4,8},{8,12},{12,16},{16,20},{20,24},{24,28},{1,5},{5,9},{9,... | collective-permute-start | bytes 393224 | tf_op jit(solution)/shard_map/ppermute | solution.py:27
  14.1 3.7 %collective-permute-done.1 = bf16[16,2,16,128]{3,2,1,0:T(8,128)(2,1)S(1)} collective-permute-done((bf16[16,2,16,128]{3,2,1,0:T(8,128)(2,1)}, bf16[16,2,16,128]{3,2,1,0:T(8,128)(2,1)S(1)}, u32[]{:S(2)}, u32[]{:S(2)}) %collective-permute-start.1) | collective-permute-done | bytes 131104 | tf_op jit(solution)/shard_map/ppermute | solution.py:29
  18.0 3.1 %collective-permute-start.2 = (bf16[16,2,48,16]{3,2,1,0:T(8,128)(2,1)S(1)}, bf16[16,2,48,16]{3,2,1,0:T(8,128)(2,1)S(1)}, u32[]{:S(2)}, u32[]{:S(2)}) collective-permute-start(bf16[16,2,48,16]{3,2,1,0:T(8,128)(2,1)S(1)} %get-tuple-element.327), channel_id=1, source_target_pairs={{0,1},{1,2},{2,3},{4,5},{5,6},{6,7},{8,9},{9,10},{10,11},{12,13},{... | collective-permute-start | bytes 147464 | tf_op jit(solution)/shard_map/ppermute | solution.py:27
  21.1 2.2 collective-permute-start.3
  23.6 5.5 %collective-permute-done.2 = bf16[16,2,48,16]{3,2,1,0:T(8,128)(2,1)S(1)} collective-permute-done((bf16[16,2,48,16]{3,2,1,0:T(8,128)(2,1)S(1)}, bf16[16,2,48,16]{3,2,1,0:T(8,128)(2,1)S(1)}, u32[]{:S(2)}, u32[]{:S(2)}) %collective-permute-start.2) | collective-permute-done | bytes 49184 | tf_op jit(solution)/shard_map/ppermute | solution.py:27
  29.0 2.8 %collective-permute-done.3 = bf16[16,2,48,16]{3,2,1,0:T(8,128)(2,1)S(1)} collective-permute-done((bf16[16,2,48,16]{3,2,1,0:T(8,128)(2,1)S(1)}, bf16[16,2,48,16]{3,2,1,0:T(8,128)(2,1)S(1)}, u32[]{:S(2)}, u32[]{:S(2)}) %collective-permute-start.3) | collective-permute-done | bytes 49184 | tf_op jit(solution)/shard_map/ppermute | solution.py:29
  31.9 1.3 pad_maximum_fusion
  33.2 95.7 %while.23 = (s32[]{:T(128)}, f32[32,32,16,8]{1,2,3,0:T(8,128)}, f32[32,32,16,8]{1,2,3,0:T(8,128)}, bf16[2,8,2,48,160]{4,3,2,1,0:T(8,128)(2,1)}, bf16[32,64]{1,0:...) while((s32[]{:T(128)}, f32[32,32,16,8]{1,2,3,0:T(8,128)}, ...), condition=%wide.region_3.4_spmd.clone, body=%wide.region_0.3_spmd.clone.sunk | while | flops 87564808 | bytes 17607756 | solution.py:151
  34.3 15.6 %while.25 = (s32[]{:T(128)}, bf16[8,48,160]{2,1,0:T(8,128)(2,1)S(1)}, s32[8,2]{0,1:T(2,128)S(1)}, bf16[8,8,36,36]{3,2,1,0:T(8,128)(2,1)S(1)}, s32[]{:T(128)}) while((s32[]{:T(128)}, bf16[8,48,160]{2,1,0:T(8,128)(2,1)S(1)}, s32[8,2]{0,1:T(2,128)S(1)}, bf16[8,8,36,36]{3,2,1,0:T(8,128)(2,1)S(1)}, s32[]{:T(128)}) %tuple.92), condition=%wide.while_cond.1, body=%wide.while_body.1.sunk | while | flops 2 | bytes 163949 | solution.py:37
  35.0 1.3 bitcast_dynamic-update-slice_fusion.5
  36.9 1.3 bitcast_dynamic-update-slice_fusion.5
  38.9 1.3 bitcast_dynamic-update-slice_fusion.5
  40.8 1.3 bitcast_dynamic-update-slice_fusion.5
  42.8 1.3 bitcast_dynamic-update-slice_fusion.5
  44.7 1.3 bitcast_dynamic-update-slice_fusion.5
  46.6 1.3 bitcast_dynamic-update-slice_fusion.5
  48.6 1.3 bitcast_dynamic-update-slice_fusion.5
  52.7 15.5 %while.24 = (s32[]{:T(128)}, bf16[8,48,160]{2,1,0:T(8,128)(2,1)S(1)}, s32[8,2]{0,1:T(2,128)S(1)}, bf16[8,8,32,32]{3,2,1,0:T(8,128)(2,1)S(1)}, s32[]{:T(128)}) while((s32[]{:T(128)}, bf16[8,48,160]{2,1,0:T(8,128)(2,1)S(1)}, s32[8,2]{0,1:T(2,128)S(1)}, bf16[8,8,32,32]{3,2,1,0:T(8,128)(2,1)S(1)}, s32[]{:T(128)}) %tuple.89), condition=%wide.while_cond, body=%wide.while_body.sunk | while | flops 2 | bytes 131181 | solution.py:37
  53.3 1.3 bitcast_dynamic-update-slice_fusion.4
  55.3 1.3 bitcast_dynamic-update-slice_fusion.4
  57.2 1.3 bitcast_dynamic-update-slice_fusion.4
  59.1 1.3 bitcast_dynamic-update-slice_fusion.4
  61.1 1.3 bitcast_dynamic-update-slice_fusion.4
  63.0 1.3 bitcast_dynamic-update-slice_fusion.4
  64.9 1.3 bitcast_dynamic-update-slice_fusion.4
  66.9 1.3 bitcast_dynamic-update-slice_fusion.4
  70.4 1.5 multiply_subtract_fusion.2
  71.8 1.4 copy.121
  73.3 2.5 bitcast_add_fusion.5
  75.8 1.4 copy.120
  77.2 1.7 bitcast_add_fusion.4
  78.9 1.3 copy-done.1
  81.3 15.6 %while.25 = (s32[]{:T(128)}, bf16[8,48,160]{2,1,0:T(8,128)(2,1)S(1)}, s32[8,2]{0,1:T(2,128)S(1)}, bf16[8,8,36,36]{3,2,1,0:T(8,128)(2,1)S(1)}, s32[]{:T(128)}) while((s32[]{:T(128)}, bf16[8,48,160]{2,1,0:T(8,128)(2,1)S(1)}, s32[8,2]{0,1:T(2,128)S(1)}, bf16[8,8,36,36]{3,2,1,0:T(8,128)(2,1)S(1)}, s32[]{:T(128)}) %tuple.92), condition=%wide.while_cond.1, body=%wide.while_body.1.sunk | while | flops 2 | bytes 163949 | solution.py:37
  82.0 1.3 bitcast_dynamic-update-slice_fusion.5
  83.9 1.3 bitcast_dynamic-update-slice_fusion.5
  85.9 1.3 bitcast_dynamic-update-slice_fusion.5
  87.8 1.3 bitcast_dynamic-update-slice_fusion.5
  89.7 1.3 bitcast_dynamic-update-slice_fusion.5
  91.7 1.3 bitcast_dynamic-update-slice_fusion.5
  93.6 1.3 bitcast_dynamic-update-slice_fusion.5
  95.6 1.3 bitcast_dynamic-update-slice_fusion.5
  99.7 15.5 %while.24 = (s32[]{:T(128)}, bf16[8,48,160]{2,1,0:T(8,128)(2,1)S(1)}, s32[8,2]{0,1:T(2,128)S(1)}, bf16[8,8,32,32]{3,2,1,0:T(8,128)(2,1)S(1)}, s32[]{:T(128)}) while((s32[]{:T(128)}, bf16[8,48,160]{2,1,0:T(8,128)(2,1)S(1)}, s32[8,2]{0,1:T(2,128)S(1)}, bf16[8,8,32,32]{3,2,1,0:T(8,128)(2,1)S(1)}, s32[]{:T(128)}) %tuple.89), condition=%wide.while_cond, body=%wide.while_body.sunk | while | flops 2 | bytes 131181 | solution.py:37
  100.3 1.3 bitcast_dynamic-update-slice_fusion.4
  102.3 1.3 bitcast_dynamic-update-slice_fusion.4
  104.2 1.3 bitcast_dynamic-update-slice_fusion.4
  106.1 1.3 bitcast_dynamic-update-slice_fusion.4
  108.1 1.3 bitcast_dynamic-update-slice_fusion.4
  110.0 1.3 bitcast_dynamic-update-slice_fusion.4
  111.9 1.3 bitcast_dynamic-update-slice_fusion.4
  117.3 1.5 multiply_subtract_fusion.2
  118.8 1.4 copy.121
  120.3 4.3 %bitcast_add_fusion.5 = f32[32,32,16,8]{1,2,3,0:T(8,128)} fusion(f32[32,32,16,8]{1,2,3,0:T(8,128)} %get-tuple-element.546, f32[32,32,8,8]{1,3,2,0:T(8,128)S(1)} %bitcast.205, pred[]{:T(512)S(6)} %compare.11, s32[8]{0:T(128)S(1)} %dynamic-slice_bitcast_fusion.2), kind=kOutput, calls=%fused_computation.7.clone.1 | convolution fusion | flops 12845184 | bytes 1310753 | tf_op jit(solution)/shard_map/while/body/eval_jaxpr/bg,jkgw->jkbw/dot_general | solution.py:142
  124.5 1.4 copy.120
  125.9 1.7 bitcast_add_fusion.4
  127.7 1.3 copy-done.1
  129.0 3.6 %copy.57 = f32[32,32,16,8]{1,3,0,2:T(8,128)} copy(f32[32,32,16,8]{1,2,3,0:T(8,128)} %get-tuple-element.169) | data formatting | bytes 1048576 | tf_op jit(solution)/shard_map/while | solution.py:151
  132.8 1.3 copy-done.2
  134.2 2.0 copy.59
  136.2 63.7 %reduce-scatter.3.cloned.1.call-done = f32[32,32,1,8]{1,3,0,2:T(8,128)} async-done(((f32[32,32,16,8]{1,3,0,2:T(8,128)}), f32[32,32,1,8]{1,3,0,2:T(8,128)}) %reduce-scatter.3.cloned.1.call-update) | async-done | bytes 32784 | tf_op jit(solution)/shard_map/reduce_scatter | solution.py:153
  199.8 1.6 fusion.40
  201.5 1.6 fusion.42
  203.1 60.9 %reduce-scatter.5.cloned.1.call-done = f32[32,32,1,8]{1,3,0,2:T(8,128)} async-done(((f32[32,32,16,8]{1,3,0,2:T(8,128)}), f32[32,32,1,8]{1,3,0,2:T(8,128)}) %reduce-scatter.5.cloned.1.call-update) | async-done | bytes 32784 | tf_op jit(solution)/shard_map/reduce_scatter | solution.py:154
  264.0 1.6 fusion.34
  265.6 1.6 fusion.35
  (146 shorter events, 39.4 us)
Async XLA Ops:
  6.5 16.9 %copy-start.5 = (s32[16]{0:T(128)S(1)}, s32[16]{0:T(128)}, u32[]{:S(2)}) copy-start(s32[16]{0:T(128)} %param.8) | copy-start | bytes 196
  6.5 193.3 %reduce-scatter.3.cloned.1.call-start = ((), (), s32[]{:S(2)}) async-start(), calls=%async_computation.2 | async-start | bytes 2228224 | tf_op jit(solution)/shard_map/reduce_scatter | solution.py:153
  6.5 6.6 %collective-permute-start = (bf16[16,2,16,128]{3,2,1,0:T(8,128)(2,1)}, bf16[16,2,16,128]{3,2,1,0:T(8,128)(2,1)S(1)}, u32[]{:S(2)}, u32[]{:S(2)}) collective-permute-start(bf16[16,2,16,128]{3,2,1,0:T(8,128)(2,1)} %param.7), channel_id=1, source_target_pairs={{0,4},{4,8},{8,12},{12,16},{16,20},{20,24},{24,28},{1,5},{5,9},{9,... | collective-permute-start | bytes 393224 | tf_op jit(solution)/shard_map/ppermute | solution.py:27
  10.7 7.1 %collective-permute-start.1 = (bf16[16,2,16,128]{3,2,1,0:T(8,128)(2,1)}, bf16[16,2,16,128]{3,2,1,0:T(8,128)(2,1)S(1)}, u32[]{:S(2)}, u32[]{:S(2)}) collective-permute-start(bf16[16,2,16,128]{3,2,1,0:T(8,128)(2,1)} %param.7), channel_id=1, source_target_pairs={{4,0},{8,4},{12,8},{16,12},{20,16},{24,20},{28,24},{5,1},{9,5},{13... | collective-permute-start | bytes 393224 | tf_op jit(solution)/shard_map/ppermute | solution.py:29
  13.2 20.1 %copy-start.3 = (bf16[32,36]{1,0:T(8,128)(2,1)S(1)}, bf16[32,36]{1,0:T(8,128)(2,1)}, u32[]{:S(2)}) copy-start(bf16[32,36]{1,0:T(8,128)(2,1)} %param.10) | copy-start | bytes 6916
  13.2 20.1 %copy-start.4 = (bf16[32,36]{1,0:T(8,128)(2,1)S(1)}, bf16[32,36]{1,0:T(8,128)(2,1)}, u32[]{:S(2)}) copy-start(bf16[32,36]{1,0:T(8,128)(2,1)} %param.11) | copy-start | bytes 6916
  18.0 11.0 %collective-permute-start.2 = (bf16[16,2,48,16]{3,2,1,0:T(8,128)(2,1)S(1)}, bf16[16,2,48,16]{3,2,1,0:T(8,128)(2,1)S(1)}, u32[]{:S(2)}, u32[]{:S(2)}) collective-permute-start(bf16[16,2,48,16]{3,2,1,0:T(8,128)(2,1)S(1)} %get-tuple-element.327), channel_id=1, source_target_pairs={{0,1},{1,2},{2,3},{4,5},{5,6},{6,7},{8,9},{9,10},{10,11},{12,13},{... | collective-permute-start | bytes 147464 | tf_op jit(solution)/shard_map/ppermute | solution.py:27
  21.1 10.8 %collective-permute-start.3 = (bf16[16,2,48,16]{3,2,1,0:T(8,128)(2,1)S(1)}, bf16[16,2,48,16]{3,2,1,0:T(8,128)(2,1)S(1)}, u32[]{:S(2)}, u32[]{:S(2)}) collective-permute-start(bf16[16,2,48,16]{3,2,1,0:T(8,128)(2,1)S(1)} %get-tuple-element.328), channel_id=1, source_target_pairs={{1,0},{2,1},{3,2},{5,4},{6,5},{7,6},{9,8},{10,9},{11,10},{13,12},{... | collective-permute-start | bytes 147464 | tf_op jit(solution)/shard_map/ppermute | solution.py:29
  73.3 3.9 %copy-start = (f32[32,32,16,8]{1,2,3,0:T(8,128)S(1)}, f32[32,32,16,8]{1,2,3,0:T(8,128)}, u32[]{:S(2)}) copy-start(f32[32,32,16,8]{1,2,3,0:T(8,128)} %get-tuple-element.545) | copy-start | bytes 1572868 | tf_op jit(solution)/shard_map/while
  78.9 1.3 copy-start.1
  120.3 5.7 %copy-start = (f32[32,32,16,8]{1,2,3,0:T(8,128)S(1)}, f32[32,32,16,8]{1,2,3,0:T(8,128)}, u32[]{:S(2)}) copy-start(f32[32,32,16,8]{1,2,3,0:T(8,128)} %get-tuple-element.545) | copy-start | bytes 1572868 | tf_op jit(solution)/shard_map/while
  127.6 1.3 copy-start.1
  132.6 1.6 copy-start.2
  132.6 131.4 %reduce-scatter.5.cloned.1.call-start = ((), (), s32[]{:S(2)}) async-start(), calls=%async_computation.3 | async-start | bytes 2228224 | tf_op jit(solution)/shard_map/reduce_scatter | solution.py:154
Sparse Core Ops, SparseCore 0:
  132.7 67.0 reduce-scatter.2
  202.7 61.2 reduce-scatter.4
where the time goes:
time: 278 us; the launch traced here: 276 us
  waiting for transfers between devices  137 us (49%)
  local copies, waits for them, and re-layouts  84.9 us (31%)
  matrix products  22.8 us (8%)
  between operations  13.5 us (5%)
  starting transfers between devices  10.9 us (4%)
  other arithmetic  6.51 us (2%)
    reduce_scatter x1, waiting for transfers between devices, body(): lax.psum_scatter(totals[0], 'tm', scatter_dimension=2, tiled=True)  63.7 us
    gather x96, local copies, waits for them, and re-layouts  61.5 us
    reduce_scatter x1, waiting for transfers between devices, body(): lax.psum_scatter(totals[1], 'tm', scatter_dimension=2, tiled=True)  60.9 us
    ppermute x2, starting transfers between devices, with_halo(): lax.ppermute(tail, axis, [(i, (i + 1) % count) for i in range(ends)])  7.24 us
    dot_general x2, matrix products, spectrum_step(): jnp.einsum('bg,jkgw->jkbw', onehot_bins, cross_imag.reshape(WIN, WIN, gro...  6.77 us
    ppermute x2, waiting for transfers between devices, with_halo(): lax.ppermute(head, axis, [((i + 1) % count, i) for i in range(ends)])  6.53 us
    ppermute x2, waiting for transfers between devices, with_halo(): lax.ppermute(tail, axis, [(i, (i + 1) % count) for i in range(ends)])  5.77 us
    while x2, local copies, waits for them, and re-layouts, body(): totals, _ = lax.scan(spectrum_step, (initial, initial), (blocks, phases))  5.6 us
  transfers between devices with their start and end apart: 6, of which 6 were waited for; matrix products, arithmetic and copies ran while one was open for 3% of the time, Pallas kernels for 0%

commit v1 on v0

v1 whole, which is shorter than its diff:
```python
import math
from functools import partial

import jax
import jax.numpy as jnp
import numpy as np
from jax import lax
from jax.experimental import pallas as pl
from jax.experimental.pallas import tpu as pltpu
from jax.sharding import PartitionSpec as P

WIN = 32
STEP = 16
BAND = 2
HALO = 16
SLOTS = WIN // 2
PATCH = WIN + 2 * BAND
SPAN = 48
GROUP = 4

F32 = jnp.float32
BF16 = jnp.bfloat16
HIGHEST = lax.Precision.HIGHEST


def dot(a, b, dims=((1,), (0,)), precision=None):
    return lax.dot_general(a, b, (dims, ((), ())), precision=precision, preferred_element_type=F32)


def tables():
    index = np.arange(WIN)
    angles = (index[:, None] * index[None, :] % WIN).astype(np.float32) * np.float32(2.0 * math.pi / WIN)
    return np.cos(angles).astype(np.float32), np.sin(angles).astype(np.float32)


def as_bf16(values):
    return np.asarray(values, np.float32).astype(jnp.bfloat16)


def constants(windows):
    cosine, sine = tables()
    cos_half = as_bf16(cosine).astype(np.float32)
    sin_half = as_bf16(sine).astype(np.float32)
    real = cos_half[:, :SLOTS]
    imag = -sin_half[:, :SLOTS]
    imag[:, 0] = cos_half[:, SLOTS]
    packed = np.concatenate([np.tile(real, (1, windows)), np.tile(imag, (1, windows))], axis=1)
    lanes = windows * SLOTS
    first = np.zeros((2 * HALO + windows * STEP, 2 * lanes), np.float32)
    for w in range(windows):
        top = HALO - (WIN - STEP) // 2 + STEP * w
        first[top : top + WIN, w * SLOTS : (w + 1) * SLOTS] = real
        first[top : top + WIN, lanes + w * SLOTS : lanes + (w + 1) * SLOTS] = imag
    rows = np.concatenate([np.tile(cos_half, (GROUP, 1)), np.tile(sin_half, (GROUP, 1))], axis=0)
    block = np.tile(np.repeat(np.arange(GROUP), WIN), 2)
    left_a = np.where(block[:, None] == np.repeat(np.arange(GROUP), WIN)[None, :], np.tile(rows, (1, GROUP)), 0.0)
    spread = np.zeros((PATCH, GROUP * SPAN), np.float32)
    for g in range(GROUP):
        spread[np.arange(PATCH), g * SPAN + np.arange(PATCH)] = 1.0
    lag = np.arange(WIN)
    back_real = 2.0 * cosine[:SLOTS]
    back_imag = -2.0 * sine[:SLOTS]
    back_real[0] = 1.0
    back_imag[0] = np.where(lag % 2 == 0, 1.0, -1.0)
    folded = np.concatenate([np.tile(back_real, (windows, 1)), np.tile(back_imag, (windows, 1))], axis=0) / WIN**3
    places = np.zeros((4, 2 * lanes, 4 * WIN), np.float32)
    for r in range(4):
        places[r, :, r * WIN : (r + 1) * WIN] = folded
    inverse_rows = np.concatenate([cosine, sine], axis=0)
    return dict(
        packed=as_bf16(packed),
        first=as_bf16(first),
        rows=as_bf16(rows),
        left_a=as_bf16(left_a),
        spread=as_bf16(spread),
        places=places,
        inverse_rows=inverse_rows,
    )


def whole(space=pltpu.VMEM):
    return pl.BlockSpec(memory_space=space)


def strips_kernel(x_ref, right_ref, left_ref):
    pairs, _, tile_rows, tile_cols = x_ref.shape
    row = lax.broadcasted_iota(jnp.int32, (2 * HALO, tile_cols), 0)
    col = lax.broadcasted_iota(jnp.int32, (2 * HALO, tile_cols), 1)
    wanted = jnp.where(row < HALO, row + (tile_cols - HALO), row - HALO)
    pick = (col == wanted).astype(F32).astype(BF16)
    span = pairs * tile_rows
    for image in range(2):
        pixels = x_ref[:, image].reshape(span, tile_cols)
        taken = dot(pick, pixels, ((1,), (1,))).astype(BF16)
        right_ref[:, image * span : (image + 1) * span] = taken[:HALO]
        left_ref[:, image * span : (image + 1) * span] = taken[HALO:]


def weights_kernel(
    shift_ref, rows_ref, cols_ref, packed_ref, table_ref, spread_ref, high_ref, low_ref, rhigh_ref, rlow_ref, wide_ref
):
    windows = shift_ref.shape[2]
    lanes = wide_ref.shape[2]
    column = dot(cols_ref[...], packed_ref[...], ((0,), (0,)))
    column = jnp.concatenate([column, jnp.zeros((40 - PATCH, 2 * lanes), F32)], axis=0)
    wide_ref[...] = jnp.zeros_like(wide_ref)
    owner = lax.broadcasted_iota(jnp.int32, (40, lanes), 1) // SLOTS
    for w in range(windows):
        start = STEP * w + HALO - (WIN - STEP) // 2 - BAND + shift_ref[1, 0, w]
        rows = pl.ds(start, 40)
        for t in range(2):
            wide_ref[t, rows, :] = jnp.where(
                owner == w, column[:, t * lanes : (t + 1) * lanes], wide_ref[t, rows, :]
            )
    total = high_ref.shape[0]
    values = jnp.concatenate([wide_ref[0, :total, :], wide_ref[1, :total, :]], axis=1)
    high = values.astype(BF16)
    high_ref[...] = high
    low_ref[...] = (values - high.astype(F32)).astype(BF16)
    spread = dot(rows_ref[...], spread_ref[...]).astype(BF16)
    left = dot(table_ref[...], spread)
    mine = (lax.broadcasted_iota(jnp.int32, left.shape, 0) // WIN) % GROUP
    theirs = lax.broadcasted_iota(jnp.int32, left.shape, 1) // SPAN
    left = jnp.where(mine == theirs, left, 0.0)
    high = left.astype(BF16)
    rhigh_ref[...] = high
    rlow_ref[...] = (left - high.astype(F32)).astype(BF16)


def spectra_kernel(
    phase_ref,
    shift_ref,
    own_ref,
    up_ref,
    down_ref,
    own_side_ref,
    up_side_ref,
    down_side_ref,
    first_ref,
    high_ref,
    low_ref,
    left_ref,
    rhigh_ref,
    rlow_ref,
    out_ref,
    half_a,
    half_b,
    sums,
):
    pairs, _, tile_rows, tile_cols = own_ref.shape
    windows = shift_ref.shape[2]
    lanes = windows * SLOTS
    span = pairs * tile_rows
    right = HALO + tile_cols

    def sides(ref, image):
        return jnp.transpose(ref[:, image * span : (image + 1) * span].astype(F32)).astype(BF16)

    def along_columns(pixels, strip, weights):
        edge = jnp.concatenate([weights[:HALO], weights[right:]], axis=0)
        return dot(pixels, weights[HALO:right]) + dot(strip, edge)

    for at, (ref, side_ref) in enumerate(
        ((up_ref, up_side_ref), (own_ref, own_side_ref), (down_ref, down_side_ref))
    ):
        place = slice(at * tile_rows, (at + 1) * tile_rows)
        pixels, strip = ref[:, 0].reshape(span, tile_cols), sides(side_ref, 0)
        half = along_columns(pixels, strip, first_ref[...])
        half_a[:, place, :] = half.reshape(pairs, tile_rows, 2 * lanes)
        pixels, strip = ref[:, 1].reshape(span, tile_cols), sides(side_ref, 1)
        half = along_columns(pixels, strip, high_ref[...]) + along_columns(pixels, strip, low_ref[...])
        for t in range(2):
            half_b[t, :, place, :] = half[:, t * lanes : (t + 1) * lanes].reshape(pairs, tile_rows, lanes)
    half_b[:, :, 3 * tile_rows :, :] = jnp.zeros((2, pairs, half_b.shape[2] - 3 * tile_rows, lanes), F32)
    sums[...] = jnp.zeros_like(sums)

    head = tile_rows - (WIN - STEP) // 2
    zero_slot = lax.broadcasted_iota(jnp.int32, (1, lanes), 1) % SLOTS == 0
    owner = lax.broadcasted_iota(jnp.int32, (1, lanes), 1) // SLOTS
    first_row = lax.broadcasted_iota(jnp.int32, (GROUP * WIN, 1), 0) % WIN == 0
    offsets = [HALO - (WIN - STEP) // 2 - BAND + shift_ref[0, 0, w] for w in range(windows)]

    def group_step(g):
        part_a, part_b = [], []
        for q in range(GROUP):
            p = g * GROUP + q
            real = half_a[p, head : head + WIN, :lanes]
            mean = jnp.sum(real, axis=0, keepdims=True) * (1.0 / WIN)
            real = real - jnp.where(zero_slot, mean, 0.0)
            part_a.append(jnp.concatenate([real, half_a[p, head : head + WIN, lanes:]], axis=1))
            lined = []
            for t in range(2):
                taken = half_b[t, p, pl.ds(offsets[0], SPAN), :]
                for w in range(1, windows):
                    taken = jnp.where(owner == w, half_b[t, p, pl.ds(offsets[w], SPAN), :], taken)
                lined.append(taken)
            part_b.append(jnp.concatenate(lined, axis=1))
        rows_a = jnp.concatenate(part_a, axis=0).astype(BF16)
        rows_b = jnp.concatenate(part_b, axis=0)
        high = rows_b.astype(BF16)
        low = (rows_b - high.astype(F32)).astype(BF16)
        spec_a = dot(left_ref[...], rows_a)
        spec_b = dot(rhigh_ref[...], high) + dot(rhigh_ref[...], low) + dot(rlow_ref[...], high)
        half_rows = GROUP * WIN
        a_cr, a_ci = spec_a[:half_rows, :lanes], spec_a[:half_rows, lanes:]
        a_sr, a_si = spec_a[half_rows:, :lanes], spec_a[half_rows:, lanes:]
        b_cr, b_ci = spec_b[:half_rows, :lanes], spec_b[:half_rows, lanes:]
        b_sr, b_si = spec_b[half_rows:, :lanes], spec_b[half_rows:, lanes:]
        b_cr = jnp.where(zero_slot & first_row, 0.0, b_cr)
        a_real, a_imag = a_cr + jnp.where(zero_slot, 0.0, a_si), jnp.where(zero_slot, 0.0, a_ci) - a_sr
        b_real, b_imag = b_cr + jnp.where(zero_slot, 0.0, b_si), jnp.where(zero_slot, 0.0, b_ci) - b_sr
        last_real = jnp.where(zero_slot, a_ci * b_ci + a_si * b_si, 0.0)
        last_imag = jnp.where(zero_slot, a_si * b_ci - a_ci * b_si, 0.0)
        cross_real = a_real * b_real + a_imag * b_imag - last_imag
        cross_imag = a_real * b_imag - a_imag * b_real + last_real
        for q in range(GROUP):
            b = phase_ref[g * GROUP + q]
            rows = slice(q * WIN, (q + 1) * WIN)
            sums[b, :, :lanes] += cross_real[rows]
            sums[b, :, lanes:] += cross_imag[rows]

    for g in range(pairs // GROUP):
        group_step(g)
    out_ref[...] = sums[...].astype(BF16)


def inverse_kernel(parts_ref, rows_ref, places_ref, out_ref, lines):
    windows = out_ref.shape[0]
    lanes = windows * SLOTS
    total = jnp.sum(parts_ref[...].astype(F32), axis=0)
    turned = dot(rows_ref[...], total, precision=HIGHEST)
    lines[:, :lanes] = turned[:WIN, :lanes] - turned[WIN:, lanes:]
    lines[:, lanes:] = turned[WIN:, :lanes] + turned[:WIN, lanes:]
    owner = (lax.broadcasted_iota(jnp.int32, (windows, 2 * lanes), 1) % lanes) // SLOTS
    own = owner == lax.broadcasted_iota(jnp.int32, (windows, 2 * lanes), 0)
    planes = None
    for r in range(4):
        spread = jnp.concatenate(
            [
                jnp.where(own, jnp.broadcast_to(lines[u : u + 1, :], (windows, 2 * lanes)), 0.0)
                for u in range(r, WIN, 4)
            ],
            axis=0,
        )
        term = dot(spread, places_ref[r], precision=HIGHEST)
        planes = term if planes is None else planes + term
    width = 4 * WIN
    for q in range(WIN // 4):
        out_ref[:, q * width : (q + 1) * width] = planes[q * windows : (q + 1) * windows]


def shifted(values, axis, step):
    count = lax.axis_size(axis)
    return lax.ppermute(values, axis, [(i, i + step) for i in range(count) if 0 <= i + step < count])


def call(kernel, outs, specs, scratch=(), flops=0, size=0):
    return pl.pallas_call(
        kernel,
        out_shape=outs,
        in_specs=specs,
        out_specs=jax.tree.map(lambda _: whole(), outs),
        scratch_shapes=scratch,
        cost_estimate=pl.CostEstimate(flops=flops, bytes_accessed=size, transcendentals=0),
    )


def body(frames, phase, shift, interp_rows, interp_cols):
    pairs, _, tile_rows, tile_cols = frames.shape
    windows = tile_cols // STEP
    lanes = windows * SLOTS
    bins = lax.axis_size("tm")
    fixed = constants(windows)
    shape = jax.ShapeDtypeStruct
    vmem, smem = whole(), whole(pltpu.SMEM)

    up = shifted(frames, "row", 1)
    down = shifted(frames, "row", -1)
    side = shape((HALO, 2 * pairs * tile_rows), BF16)
    rightward, leftward = call(strips_kernel, (side, side), [vmem], flops=10**7, size=200000)(frames)
    own_side = jnp.concatenate([shifted(rightward, "col", 1), shifted(leftward, "col", -1)], axis=0)
    up_side = shifted(own_side, "row", 1)
    down_side = shifted(own_side, "row", -1)

    wide = 2 * HALO + tile_cols
    high, low, rhigh, rlow = call(
        weights_kernel,
        (
            shape((wide, 2 * lanes), BF16),
            shape((wide, 2 * lanes), BF16),
            shape((2 * GROUP * WIN, GROUP * SPAN), BF16),
            shape((2 * GROUP * WIN, GROUP * SPAN), BF16),
        ),
        [smem] + [vmem] * 5,
        scratch=[pltpu.VMEM((2, wide + 8, lanes), F32)],
        flops=10**7,
        size=400000,
    )(shift, interp_rows, interp_cols, fixed["packed"], fixed["rows"], fixed["spread"])

    partial_sums = call(
        spectra_kernel,
        shape((bins, WIN, 2 * lanes), BF16),
        [smem, smem] + [vmem] * 12,
        scratch=[
            pltpu.VMEM((pairs, SPAN, 2 * lanes), F32),
            pltpu.VMEM((2, pairs, SPAN + 16, lanes), F32),
            pltpu.VMEM((bins, WIN, 2 * lanes), F32),
        ],
        flops=10**9,
        size=10**6,
    )(
        phase,
        shift,
        frames,
        up,
        down,
        own_side,
        up_side,
        down_side,
        fixed["first"],
        high,
        low,
        fixed["left_a"],
        rhigh,
        rlow,
    )
    parts = lax.all_to_all(partial_sums, "tm", 0, 0, tiled=True)
    planes = call(
        inverse_kernel,
        shape((windows, WIN * WIN), F32),
        [vmem] * 3,
        scratch=[pltpu.VMEM((WIN, 2 * lanes), F32)],
        flops=10**8,
        size=10**6,
    )(parts, fixed["inverse_rows"], fixed["places"])
    return planes[None, None]


def solution(mesh):
    placed = (P("tm", None, "row", "col"), P("tm"), P(None, "row", "col"), P(), P())
    return jax.shard_map(
        body, mesh=mesh, in_specs=placed, out_specs=P("tm", "row", "col", None), check_vma=False
    )
```

time: 278 us -> 54.5 us (0.20)
  the two profiles are of different devices: /device:TPU:27 before, /device:TPU:193 now
where the time goes in v1:
time: 54.5 us; the launch traced here: 54 us
  blocking collectives  21.7 us (40%)
  starting transfers between devices  18 us (33%)
  Pallas kernels  10.1 us (19%)
  waiting for transfers between devices  3.38 us (6%)
  local copies, waits for them, and re-layouts  0.69 us (1%)
    all_to_all x1, blocking collectives, body(): parts = lax.all_to_all(partial_sums, 'tm', 0, 0, tiled=True)  21.7 us
    ppermute x6, starting transfers between devices, shifted(): lax.ppermute(values, axis, [(i, i + step) for i in range(count) if 0 <= i...  18 us
    pallas_call x1, Pallas kernels, body(): call(spectra_kernel, shape((bins, WIN, 2 * lanes), BF16), [smem, smem] +...  3.99 us
    ppermute x6, waiting for transfers between devices, shifted(): lax.ppermute(values, axis, [(i, i + step) for i in range(count) if 0 <= i...  3.38 us
    pallas_call x1, Pallas kernels, body(): call(inverse_kernel, shape((windows, WIN * WIN), F32), [vmem] * 3, scratc...  2.42 us
    pallas_call x1, Pallas kernels, body(): call(weights_kernel, (shape((wide, 2 * lanes), BF16), shape((wide, 2 * la...  1.94 us
    pallas_call x1, Pallas kernels, body(): call(strips_kernel, (side, side), [vmem], flops=10 ** 7, size=200000)  1.74 us
  transfers between devices with their start and end apart: 6, of which 1 were waited for; matrix products, arithmetic and copies ran while one was open for 0% of the time, Pallas kernels for 4%

profile of v1, /device:TPU:193, one launch (start us, length us, event | category | flops | bytes accessed | tf_op | source)
XLA Modules:
  0.0 54.0 jit_solution(10096463630968369890)
XLA Ops:
  0.0 0.0 copy-start
  0.0 1.7 %shard_map.118 = (bf16[16,512]{1,0:T(8,128)(2,1)}, bf16[16,512]{1,0:T(8,128)(2,1)}) custom-call(bf16[16,2,16,128]{3,2,1,0:T(8,128)(2,1)} %own_ref.1), custom_call_target="tpu_custom_call" | custom-call | flops 10000000 | bytes 200000 | tf_op jit(solution)/shard_map/pallas_call | solution.py:280
  1.7 3.1 %collective-permute-start.2 = (bf16[16,512]{1,0:T(8,128)(2,1)}, bf16[16,512]{1,0:T(8,128)(2,1)S(1)}, u32[]{:S(2)}, u32[]{:S(2)}) collective-permute-start(bf16[16,512]{1,0:T(8,128)(2,1)} %get-tuple-element.11), channel_id=1, source_target_pairs={{0,1},{1,2},{2,3},{4,5},{5,6},{6,7},{8,9},{9,10},{10,11},{12,13},{... | collective-permute-start | bytes 49160 | tf_op jit(solution)/shard_map/ppermute | solution.py:254
  4.8 0.0 copy-done
  4.9 1.9 %collective-permute-start.1 = (bf16[16,2,16,128]{3,2,1,0:T(8,128)(2,1)S(1)}, bf16[16,2,16,128]{3,2,1,0:T(8,128)(2,1)S(1)}, u32[]{:S(2)}, u32[]{:S(2)}) collective-permute-start(bf16[16,2,16,128]{3,2,1,0:T(8,128)(2,1)S(1)} %copy-done), channel_id=1, source_target_pairs={{4,0},{8,4},{12,8},{16,12},{20,16},{24,20},{28,24},{5,1},{9,5},{13... | collective-permute-start | bytes 393224 | tf_op jit(solution)/shard_map/ppermute | solution.py:254
  6.8 5.2 %collective-permute-start = (bf16[16,2,16,128]{3,2,1,0:T(8,128)(2,1)S(1)}, bf16[16,2,16,128]{3,2,1,0:T(8,128)(2,1)S(1)}, u32[]{:S(2)}, u32[]{:S(2)}) collective-permute-start(bf16[16,2,16,128]{3,2,1,0:T(8,128)(2,1)S(1)} %copy-done), channel_id=1, source_target_pairs={{0,4},{4,8},{8,12},{12,16},{16,20},{20,24},{24,28},{1,5},{5,9},{9,... | collective-permute-start | bytes 393224 | tf_op jit(solution)/shard_map/ppermute | solution.py:254
  12.0 1.3 %collective-permute-start.3 = (bf16[16,512]{1,0:T(8,128)(2,1)}, bf16[16,512]{1,0:T(8,128)(2,1)S(1)}, u32[]{:S(2)}, u32[]{:S(2)}) collective-permute-start(bf16[16,512]{1,0:T(8,128)(2,1)} %get-tuple-element.12), channel_id=1, source_target_pairs={{1,0},{2,1},{3,2},{5,4},{6,5},{7,6},{9,8},{10,9},{11,10},{13,12},{... | collective-permute-start | bytes 49160 | tf_op jit(solution)/shard_map/ppermute | solution.py:254
  13.3 0.0 collective-permute-done.2
  13.3 3.4 %collective-permute-done.3 = bf16[16,512]{1,0:T(8,128)(2,1)S(1)} collective-permute-done((bf16[16,512]{1,0:T(8,128)(2,1)}, bf16[16,512]{1,0:T(8,128)(2,1)S(1)}, u32[]{:S(2)}, u32[]{:S(2)}) %collective-permute-start.3) | collective-permute-done | bytes 16416 | tf_op jit(solution)/shard_map/ppermute | solution.py:254
  16.7 0.0 copy-start.1
  16.7 1.9 %collective-permute-start.5 = (bf16[32,512]{1,0:T(8,128)(2,1)S(1)}, bf16[32,512]{1,0:T(8,128)(2,1)S(1)}, u32[]{:S(2)}, u32[]{:S(2)}) collective-permute-start(bf16[32,512]{1,0:T(8,128)(2,1)S(1)} %constant_dynamic-update-slice_fusion.own_side_ref), channel_id=1, source_target_pairs={{4,0},{8,4},{12,8},{16,12},{20,16},{24,20},{28,24},{5,1},{9,5},{13... | collective-permute-start | bytes 98312 | tf_op jit(solution)/shard_map/ppermute | solution.py:254
  18.6 4.6 %collective-permute-start.4 = (bf16[32,512]{1,0:T(8,128)(2,1)S(1)}, bf16[32,512]{1,0:T(8,128)(2,1)S(1)}, u32[]{:S(2)}, u32[]{:S(2)}) collective-permute-start(bf16[32,512]{1,0:T(8,128)(2,1)S(1)} %constant_dynamic-update-slice_fusion.own_side_ref), channel_id=1, source_target_pairs={{0,4},{4,8},{8,12},{12,16},{16,20},{20,24},{24,28},{1,5},{5,9},{9,... | collective-permute-start | bytes 98312 | tf_op jit(solution)/shard_map/ppermute | solution.py:254
  23.2 1.9 %shard_map.119 = (bf16[160,256]{1,0:T(8,128)(2,1)}, bf16[160,256]{1,0:T(8,128)(2,1)}, bf16[256,192]{1,0:T(8,128)(2,1)}, bf16[256,192]{1,0:T(8,128)(2,1)}) custom-call(s32[2,1,8]{2,1,0:T(1,128)} %shift_ref.3, bf16[32,36]{1,0:T(8,128)(2,1)} %rows_ref.2, bf16[32,36]{1,0:T(8,128)(2,1)} %cols_ref.1, bf16[32,256]{1,0:T(8,128)(2,1)} %constant.14.clone.packed_ref, ...), custom_call_target="tpu_custom_call" | custom-call | flops 10000000 | bytes 400000 | tf_op jit(solution)/shard_map/pallas_call | solution.py:286
  25.1 0.0 copy-done.1
  25.1 0.0 collective-permute-done.5.down_side_ref
  25.1 0.0 copy-start.4
  25.2 0.0 collective-permute-done.4.up_side_ref
  25.2 0.0 copy-start.5
  25.2 0.0 collective-permute-done.1.down_ref
  25.2 0.0 copy-start.2
  25.2 0.0 collective-permute-done.up_ref
  25.2 0.0 copy-start.3
  25.2 0.5 copy-done.4
  25.8 0.0 copy-done.5
  25.8 0.1 copy-done.2
  25.8 0.1 copy-done.3
  25.9 4.0 %shard_map.120 = bf16[16,32,256]{2,1,0:T(8,128)(2,1)} custom-call(s32[16]{0:T(128)} %phase_ref.1, s32[2,1,8]{2,1,0:T(1,128)} %shift_ref.3, bf16[16,2,16,128]{3,2,1,0:T(8,128)(2,1)} %own_ref.1, bf16[16,2,16,128]{3,2,1,0:T(8,128)(2,1)} %copy-done.3, bf16[16,2,16,128]{3,2,1,0:T(8,128)(2,1)} %copy-done.2, bf16[32,512]{1,0:T(8,128)(2,1)} %copy-done.1, ...), custom_call_target="tpu_custom_call" | custom-call | flops 1000000000 | bytes 1000000 | tf_op jit(solution)/shard_map/pallas_call | solution.py:300
  29.9 21.7 %all_to_all.5.parts_ref = bf16[16,32,256]{2,1,0:T(8,128)(2,1)} all-to-all(bf16[16,32,256]{2,1,0:T(8,128)(2,1)} %shard_map.120), channel_id=1, replica_groups=mesh['tm'=16,'row'=8,'col'=4] {'tm'}, dimensions={0} | all-to-all | bytes 524288 | tf_op jit(solution)/shard_map/all_to_all | solution.py:327
  51.6 2.4 %shard_map.121 = f32[8,1024]{1,0:T(8,128)} custom-call(bf16[16,32,256]{2,1,0:T(8,128)(2,1)} %all_to_all.5.parts_ref, f32[64,32]{1,0:T(8,128)} %constant.19.clone.rows_ref, f32[4,256,128]{2,1,0:T(8,128)} %constant.20.clone.places_ref), custom_call_target="tpu_custom_call" | custom-call | flops 100000000 | bytes 1000000 | tf_op jit(solution)/shard_map/pallas_call | solution.py:328
  (2 shorter events, 0.0 us)
Async XLA Ops:
  0.0 4.9 %copy-start = (bf16[16,2,16,128]{3,2,1,0:T(8,128)(2,1)S(1)}, bf16[16,2,16,128]{3,2,1,0:T(8,128)(2,1)}, u32[]{:S(2)}) copy-start(bf16[16,2,16,128]{3,2,1,0:T(8,128)(2,1)} %own_ref.1) | copy-start | bytes 393220
  1.7 11.6 %collective-permute-start.2 = (bf16[16,512]{1,0:T(8,128)(2,1)}, bf16[16,512]{1,0:T(8,128)(2,1)S(1)}, u32[]{:S(2)}, u32[]{:S(2)}) collective-permute-start(bf16[16,512]{1,0:T(8,128)(2,1)} %get-tuple-element.11), channel_id=1, source_target_pairs={{0,1},{1,2},{2,3},{4,5},{5,6},{6,7},{8,9},{9,10},{10,11},{12,13},{... | collective-permute-start | bytes 49160 | tf_op jit(solution)/shard_map/ppermute | solution.py:254
  4.9 20.3 %collective-permute-start.1 = (bf16[16,2,16,128]{3,2,1,0:T(8,128)(2,1)S(1)}, bf16[16,2,16,128]{3,2,1,0:T(8,128)(2,1)S(1)}, u32[]{:S(2)}, u32[]{:S(2)}) collective-permute-start(bf16[16,2,16,128]{3,2,1,0:T(8,128)(2,1)S(1)} %copy-done), channel_id=1, source_target_pairs={{4,0},{8,4},{12,8},{16,12},{20,16},{24,20},{28,24},{5,1},{9,5},{13... | collective-permute-start | bytes 393224 | tf_op jit(solution)/shard_map/ppermute | solution.py:254
  6.8 18.4 %collective-permute-start = (bf16[16,2,16,128]{3,2,1,0:T(8,128)(2,1)S(1)}, bf16[16,2,16,128]{3,2,1,0:T(8,128)(2,1)S(1)}, u32[]{:S(2)}, u32[]{:S(2)}) collective-permute-start(bf16[16,2,16,128]{3,2,1,0:T(8,128)(2,1)S(1)} %copy-done), channel_id=1, source_target_pairs={{0,4},{4,8},{8,12},{12,16},{16,20},{20,24},{24,28},{1,5},{5,9},{9,... | collective-permute-start | bytes 393224 | tf_op jit(solution)/shard_map/ppermute | solution.py:254
  12.0 4.7 %collective-permute-start.3 = (bf16[16,512]{1,0:T(8,128)(2,1)}, bf16[16,512]{1,0:T(8,128)(2,1)S(1)}, u32[]{:S(2)}, u32[]{:S(2)}) collective-permute-start(bf16[16,512]{1,0:T(8,128)(2,1)} %get-tuple-element.12), channel_id=1, source_target_pairs={{1,0},{2,1},{3,2},{5,4},{6,5},{7,6},{9,8},{10,9},{11,10},{13,12},{... | collective-permute-start | bytes 49160 | tf_op jit(solution)/shard_map/ppermute | solution.py:254
  16.7 8.4 %copy-start.1 = (bf16[32,512]{1,0:T(8,128)(2,1)}, bf16[32,512]{1,0:T(8,128)(2,1)S(1)}, u32[]{:S(2)}) copy-start(bf16[32,512]{1,0:T(8,128)(2,1)S(1)} %constant_dynamic-update-slice_fusion.own_side_ref) | copy-start | bytes 98308
  16.7 8.4 %collective-permute-start.5 = (bf16[32,512]{1,0:T(8,128)(2,1)S(1)}, bf16[32,512]{1,0:T(8,128)(2,1)S(1)}, u32[]{:S(2)}, u32[]{:S(2)}) collective-permute-start(bf16[32,512]{1,0:T(8,128)(2,1)S(1)} %constant_dynamic-update-slice_fusion.own_side_ref), channel_id=1, source_target_pairs={{4,0},{8,4},{12,8},{16,12},{20,16},{24,20},{28,24},{5,1},{9,5},{13... | collective-permute-start | bytes 98312 | tf_op jit(solution)/shard_map/ppermute | solution.py:254
  18.6 6.5 %collective-permute-start.4 = (bf16[32,512]{1,0:T(8,128)(2,1)S(1)}, bf16[32,512]{1,0:T(8,128)(2,1)S(1)}, u32[]{:S(2)}, u32[]{:S(2)}) collective-permute-start(bf16[32,512]{1,0:T(8,128)(2,1)S(1)} %constant_dynamic-update-slice_fusion.own_side_ref), channel_id=1, source_target_pairs={{0,4},{4,8},{8,12},{12,16},{16,20},{20,24},{24,28},{1,5},{5,9},{9,... | collective-permute-start | bytes 98312 | tf_op jit(solution)/shard_map/ppermute | solution.py:254
  25.1 0.6 %copy-start.4 = (bf16[32,512]{1,0:T(8,128)(2,1)}, bf16[32,512]{1,0:T(8,128)(2,1)S(1)}, u32[]{:S(2)}) copy-start(bf16[32,512]{1,0:T(8,128)(2,1)S(1)} %collective-permute-done.5.down_side_ref) | copy-start | bytes 98308
  25.2 0.6 %copy-start.5 = (bf16[32,512]{1,0:T(8,128)(2,1)}, bf16[32,512]{1,0:T(8,128)(2,1)S(1)}, u32[]{:S(2)}) copy-start(bf16[32,512]{1,0:T(8,128)(2,1)S(1)} %collective-permute-done.4.up_side_ref) | copy-start | bytes 98308
  25.2 0.6 %copy-start.2 = (bf16[16,2,16,128]{3,2,1,0:T(8,128)(2,1)}, bf16[16,2,16,128]{3,2,1,0:T(8,128)(2,1)S(1)}, u32[]{:S(2)}) copy-start(bf16[16,2,16,128]{3,2,1,0:T(8,128)(2,1)S(1)} %collective-permute-done.1.down_ref) | copy-start | bytes 393220
  25.2 0.7 %copy-start.3 = (bf16[16,2,16,128]{3,2,1,0:T(8,128)(2,1)}, bf16[16,2,16,128]{3,2,1,0:T(8,128)(2,1)S(1)}, u32[]{:S(2)}) copy-start(bf16[16,2,16,128]{3,2,1,0:T(8,128)(2,1)S(1)} %collective-permute-done.up_ref) | copy-start | bytes 393220

commit v2 on v1

--- a/solution.py
+++ b/solution.py
@@ -63,9 +63,6 @@
     back_real[0] = 1.0
     back_imag[0] = np.where(lag % 2 == 0, 1.0, -1.0)
     folded = np.concatenate([np.tile(back_real, (windows, 1)), np.tile(back_imag, (windows, 1))], axis=0) / WIN**3
-    places = np.zeros((4, 2 * lanes, 4 * WIN), np.float32)
-    for r in range(4):
-        places[r, :, r * WIN : (r + 1) * WIN] = folded
     inverse_rows = np.concatenate([cosine, sine], axis=0)
     return dict(
         packed=as_bf16(packed),
@@ -73,7 +70,7 @@
         rows=as_bf16(rows),
         left_a=as_bf16(left_a),
         spread=as_bf16(spread),
-        places=places,
+        places=folded,
         inverse_rows=inverse_rows,
     )
 
@@ -82,18 +79,20 @@
     return pl.BlockSpec(memory_space=space)
 
 
-def strips_kernel(x_ref, right_ref, left_ref):
-    pairs, _, tile_rows, tile_cols = x_ref.shape
+def strips_kernel(up_ref, own_ref, down_ref, right_ref, left_ref):
+    pairs, _, tile_rows, tile_cols = own_ref.shape
     row = lax.broadcasted_iota(jnp.int32, (2 * HALO, tile_cols), 0)
     col = lax.broadcasted_iota(jnp.int32, (2 * HALO, tile_cols), 1)
     wanted = jnp.where(row < HALO, row + (tile_cols - HALO), row - HALO)
     pick = (col == wanted).astype(F32).astype(BF16)
     span = pairs * tile_rows
-    for image in range(2):
-        pixels = x_ref[:, image].reshape(span, tile_cols)
-        taken = dot(pick, pixels, ((1,), (1,))).astype(BF16)
-        right_ref[:, image * span : (image + 1) * span] = taken[:HALO]
-        left_ref[:, image * span : (image + 1) * span] = taken[HALO:]
+    for at, ref in enumerate((up_ref, own_ref, down_ref)):
+        for image in range(2):
+            pixels = ref[:, image].reshape(span, tile_cols)
+            taken = dot(pick, pixels, ((1,), (1,))).astype(BF16)
+            place = slice((2 * at + image) * span, (2 * at + image + 1) * span)
+            right_ref[:, place] = taken[:HALO]
+            left_ref[:, place] = taken[HALO:]
 
 
 def weights_kernel(
@@ -133,9 +132,8 @@
     own_ref,
     up_ref,
     down_ref,
-    own_side_ref,
-    up_side_ref,
-    down_side_ref,
+    before_ref,
+    after_ref,
     first_ref,
     high_ref,
     low_ref,
@@ -153,24 +151,24 @@
     span = pairs * tile_rows
     right = HALO + tile_cols
 
-    def sides(ref, image):
-        return jnp.transpose(ref[:, image * span : (image + 1) * span].astype(F32)).astype(BF16)
-
     def along_columns(pixels, strip, weights):
         edge = jnp.concatenate([weights[:HALO], weights[right:]], axis=0)
         return dot(pixels, weights[HALO:right]) + dot(strip, edge)
 
-    for at, (ref, side_ref) in enumerate(
-        ((up_ref, up_side_ref), (own_ref, own_side_ref), (down_ref, down_side_ref))
-    ):
-        place = slice(at * tile_rows, (at + 1) * tile_rows)
-        pixels, strip = ref[:, 0].reshape(span, tile_cols), sides(side_ref, 0)
-        half = along_columns(pixels, strip, first_ref[...])
-        half_a[:, place, :] = half.reshape(pairs, tile_rows, 2 * lanes)
-        pixels, strip = ref[:, 1].reshape(span, tile_cols), sides(side_ref, 1)
-        half = along_columns(pixels, strip, high_ref[...]) + along_columns(pixels, strip, low_ref[...])
+    for at, ref in enumerate((up_ref, own_ref, down_ref)):
+        rows = slice(at * tile_rows, (at + 1) * tile_rows)
+        strips = []
+        for image in range(2):
+            place = slice((2 * at + image) * span, (2 * at + image + 1) * span)
+            strip = jnp.concatenate([before_ref[:, place], after_ref[:, place]], axis=0)
+            strips.append(jnp.transpose(strip.astype(F32)).astype(BF16))
+        pixels = ref[:, 0].reshape(span, tile_cols)
+        half = along_columns(pixels, strips[0], first_ref[...])
+        half_a[:, rows, :] = half.reshape(pairs, tile_rows, 2 * lanes)
+        pixels = ref[:, 1].reshape(span, tile_cols)
+        half = along_columns(pixels, strips[1], high_ref[...]) + along_columns(pixels, strips[1], low_ref[...])
         for t in range(2):
-            half_b[t, :, place, :] = half[:, t * lanes : (t + 1) * lanes].reshape(pairs, tile_rows, lanes)
+            half_b[t, :, rows, :] = half[:, t * lanes : (t + 1) * lanes].reshape(pairs, tile_rows, lanes)
     half_b[:, :, 3 * tile_rows :, :] = jnp.zeros((2, pairs, half_b.shape[2] - 3 * tile_rows, lanes), F32)
     sums[...] = jnp.zeros_like(sums)
 
@@ -233,20 +231,13 @@
     lines[:, lanes:] = turned[WIN:, :lanes] + turned[:WIN, lanes:]
     owner = (lax.broadcasted_iota(jnp.int32, (windows, 2 * lanes), 1) % lanes) // SLOTS
     own = owner == lax.broadcasted_iota(jnp.int32, (windows, 2 * lanes), 0)
-    planes = None
-    for r in range(4):
-        spread = jnp.concatenate(
-            [
-                jnp.where(own, jnp.broadcast_to(lines[u : u + 1, :], (windows, 2 * lanes)), 0.0)
-                for u in range(r, WIN, 4)
-            ],
-            axis=0,
-        )
-        term = dot(spread, places_ref[r], precision=HIGHEST)
-        planes = term if planes is None else planes + term
-    width = 4 * WIN
-    for q in range(WIN // 4):
-        out_ref[:, q * width : (q + 1) * width] = planes[q * windows : (q + 1) * windows]
+    spread = jnp.concatenate(
+        [jnp.where(own, jnp.broadcast_to(lines[u : u + 1, :], (windows, 2 * lanes)), 0.0) for u in range(WIN)],
+        axis=0,
+    )
+    planes = dot(spread, places_ref[...], precision=HIGHEST)
+    for u in range(WIN):
+        out_ref[:, u * WIN : (u + 1) * WIN] = planes[u * windows : (u + 1) * windows]
 
 
 def shifted(values, axis, step):
@@ -254,13 +245,14 @@
     return lax.ppermute(values, axis, [(i, i + step) for i in range(count) if 0 <= i + step < count])
 
 
-def call(kernel, outs, specs, scratch=(), flops=0, size=0):
+def call(kernel, outs, specs, scratch=(), flops=0, size=0, room=16):
     return pl.pallas_call(
         kernel,
         out_shape=outs,
         in_specs=specs,
         out_specs=jax.tree.map(lambda _: whole(), outs),
         scratch_shapes=scratch,
+        compiler_params=pltpu.CompilerParams(vmem_limit_bytes=room << 20),
         cost_estimate=pl.CostEstimate(flops=flops, bytes_accessed=size, transcendentals=0),
     )
 
@@ -276,11 +268,10 @@
 
     up = shifted(frames, "row", 1)
     down = shifted(frames, "row", -1)
-    side = shape((HALO, 2 * pairs * tile_rows), BF16)
-    rightward, leftward = call(strips_kernel, (side, side), [vmem], flops=10**7, size=200000)(frames)
-    own_side = jnp.concatenate([shifted(rightward, "col", 1), shifted(leftward, "col", -1)], axis=0)
-    up_side = shifted(own_side, "row", 1)
-    down_side = shifted(own_side, "row", -1)
+    side = shape((HALO, 6 * pairs * tile_rows), BF16)
+    rightward, leftward = call(strips_kernel, (side, side), [vmem] * 3, flops=10**7, size=200000)(up, frames, down)
+    before = shifted(rightward, "col", 1)
+    after = shifted(leftward, "col", -1)
 
     wide = 2 * HALO + tile_cols
     high, low, rhigh, rlow = call(
@@ -300,7 +291,7 @@
     partial_sums = call(
         spectra_kernel,
         shape((bins, WIN, 2 * lanes), BF16),
-        [smem, smem] + [vmem] * 12,
+        [smem, smem] + [vmem] * 11,
         scratch=[
             pltpu.VMEM((pairs, SPAN, 2 * lanes), F32),
             pltpu.VMEM((2, pairs, SPAN + 16, lanes), F32),
@@ -314,9 +305,8 @@
         frames,
         up,
         down,
-        own_side,
-        up_side,
-        down_side,
+        before,
+        after,
         fixed["first"],
         high,
         low,

time: 54.5 us -> 44.7 us (0.82)
  the two profiles are of different devices: /device:TPU:193 before, /device:TPU:259 now
where the time goes in v2:
time: 44.7 us; the launch traced here: 44.5 us
  blocking collectives  21.6 us (48%)
  starting transfers between devices  10.7 us (24%)
  waiting for transfers between devices  6 us (13%)
  Pallas kernels  5.01 us (11%)
  local copies, waits for them, and re-layouts  0.97 us (2%)
    all_to_all x1, blocking collectives, body(): parts = lax.all_to_all(partial_sums, 'tm', 0, 0, tiled=True)  21.6 us
    ppermute x4, starting transfers between devices, shifted(): lax.ppermute(values, axis, [(i, i + step) for i in range(count) if 0 <= i...  10.7 us
    ppermute x4, waiting for transfers between devices, shifted(): lax.ppermute(values, axis, [(i, i + step) for i in range(count) if 0 <= i...  6 us
    pallas_call x1, Pallas kernels, body(): call(spectra_kernel, shape((bins, WIN, 2 * lanes), BF16), [smem, smem] +...  2.56 us
    pallas_call x1, Pallas kernels, body(): call(inverse_kernel, shape((windows, WIN * WIN), F32), [vmem] * 3, scratc...  1.34 us
    unnamed x26, local copies, waits for them, and re-layouts  0.97 us
    pallas_call x1, Pallas kernels, body(): call(weights_kernel, (shape((wide, 2 * lanes), BF16), shape((wide, 2 * la...  0.91 us
  transfers between devices with their start and end apart: 4, of which 3 were waited for; matrix products, arithmetic and copies ran while one was open for 0% of the time, Pallas kernels for 2%

profile of v2, /device:TPU:259, one launch (start us, length us, event | category | flops | bytes accessed | tf_op | source)
XLA Modules:
  0.0 44.5 jit_solution(13951909558000130385)
XLA Ops:
  0.0 1.9 %collective-permute-start.1 = (bf16[16,2,16,128]{3,2,1,0:T(8,128)(2,1)}, bf16[16,2,16,128]{3,2,1,0:T(8,128)(2,1)S(1)}, u32[]{:S(2)}, u32[]{:S(2)}) collective-permute-start(bf16[16,2,16,128]{3,2,1,0:T(8,128)(2,1)} %own_ref.3), channel_id=1, source_target_pairs={{4,0},{8,4},{12,8},{16,12},{20,16},{24,20},{28,24},{5,1},{9,5},{13... | collective-permute-start | bytes 393224 | tf_op jit(solution)/shard_map/ppermute | solution.py:245
  1.9 3.4 %collective-permute-start = (bf16[16,2,16,128]{3,2,1,0:T(8,128)(2,1)}, bf16[16,2,16,128]{3,2,1,0:T(8,128)(2,1)S(1)}, u32[]{:S(2)}, u32[]{:S(2)}) collective-permute-start(bf16[16,2,16,128]{3,2,1,0:T(8,128)(2,1)} %own_ref.3), channel_id=1, source_target_pairs={{0,4},{4,8},{8,12},{12,16},{16,20},{20,24},{24,28},{1,5},{5,9},{9,... | collective-permute-start | bytes 393224 | tf_op jit(solution)/shard_map/ppermute | solution.py:245
  5.3 1.2 %collective-permute-done.1.down_ref = bf16[16,2,16,128]{3,2,1,0:T(8,128)(2,1)S(1)} collective-permute-done((bf16[16,2,16,128]{3,2,1,0:T(8,128)(2,1)}, bf16[16,2,16,128]{3,2,1,0:T(8,128)(2,1)S(1)}, u32[]{:S(2)}, u32[]{:S(2)}) %collective-permute-start.1) | collective-permute-done | bytes 131104 | tf_op jit(solution)/shard_map/ppermute | solution.py:245
  6.5 3.1 %collective-permute-done.up_ref = bf16[16,2,16,128]{3,2,1,0:T(8,128)(2,1)S(1)} collective-permute-done((bf16[16,2,16,128]{3,2,1,0:T(8,128)(2,1)}, bf16[16,2,16,128]{3,2,1,0:T(8,128)(2,1)S(1)}, u32[]{:S(2)}, u32[]{:S(2)}) %collective-permute-start) | collective-permute-done | bytes 131104 | tf_op jit(solution)/shard_map/ppermute | solution.py:245
  9.6 0.0 copy-start
  9.6 0.9 %copy-done = bf16[16,2,16,128]{3,2,1,0:T(8,128)(2,1)S(1)} copy-done((bf16[16,2,16,128]{3,2,1,0:T(8,128)(2,1)S(1)}, bf16[16,2,16,128]{3,2,1,0:T(8,128)(2,1)}, u32[]{:S(2)}) %copy-start) | copy-done | bytes 131096
  10.5 0.0 copy-start.3
  10.5 0.0 copy-start.5
  10.5 0.0 copy-start.6
  10.5 0.0 copy-start.7
  10.5 0.0 copy-start.8
  10.5 0.0 copy-start.9
  10.6 0.0 copy-start.10
  10.6 0.0 copy-start.11
  10.6 0.0 copy-start.12
  10.6 0.2 shard_map.118
  10.8 0.0 copy-start.1
  10.8 3.3 %collective-permute-start.2 = (bf16[16,1536]{1,0:T(8,128)(2,1)S(1)}, bf16[16,1536]{1,0:T(8,128)(2,1)S(1)}, u32[]{:S(2)}, u32[]{:S(2)}) collective-permute-start(bf16[16,1536]{1,0:T(8,128)(2,1)S(1)} %get-tuple-element.11), channel_id=1, source_target_pairs={{0,1},{1,2},{2,3},{4,5},{5,6},{6,7},{8,9},{9,10},{10,11},{12,13},{... | collective-permute-start | bytes 147464 | tf_op jit(solution)/shard_map/ppermute | solution.py:245
  14.1 2.2 %collective-permute-start.3 = (bf16[16,1536]{1,0:T(8,128)(2,1)S(1)}, bf16[16,1536]{1,0:T(8,128)(2,1)S(1)}, u32[]{:S(2)}, u32[]{:S(2)}) collective-permute-start(bf16[16,1536]{1,0:T(8,128)(2,1)S(1)} %get-tuple-element.12), channel_id=1, source_target_pairs={{1,0},{2,1},{3,2},{5,4},{6,5},{7,6},{9,8},{10,9},{11,10},{13,12},{... | collective-permute-start | bytes 147464 | tf_op jit(solution)/shard_map/ppermute | solution.py:245
  16.2 0.0 copy-done.3
  16.3 0.0 copy-done.5
  16.3 0.0 copy-done.6
  16.3 0.0 copy-done.7
  16.3 0.0 copy-done.8
  16.3 0.0 copy-done.9
  16.3 0.9 %shard_map.119 = (bf16[160,256]{1,0:T(8,128)(2,1)S(1)}, bf16[160,256]{1,0:T(8,128)(2,1)S(1)}, bf16[256,192]{1,0:T(8,128)(2,1)S(1)}, bf16[256,192]{1,0:T(8,128)(2,1)S(1)}) custom-call(s32[2,1,8]{2,1,0:T(1,128)S(1)} %copy-done.9, bf16[32,36]{1,0:T(8,128)(2,1)S(1)} %copy-done.7, bf16[32,36]{1,0:T(8,128)(2,1)S(1)} %copy-done.8, bf16[32,256]{1,0:T(8,128)(2,1)S(1)} %copy-done.6, ...), custom_call_target="tpu_custom_call" | custom-call | flops 10000000 | bytes 400000 | tf_op jit(solution)/shard_map/pallas_call | solution.py:277
  17.2 0.0 collective-permute-done.2.before_ref
  17.2 1.7 %collective-permute-done.3.after_ref = bf16[16,1536]{1,0:T(8,128)(2,1)S(1)} collective-permute-done((bf16[16,1536]{1,0:T(8,128)(2,1)S(1)}, bf16[16,1536]{1,0:T(8,128)(2,1)S(1)}, u32[]{:S(2)}, u32[]{:S(2)}) %collective-permute-start.3) | collective-permute-done | bytes 49184 | tf_op jit(solution)/shard_map/ppermute | solution.py:245
  18.9 0.0 copy-done.10
  18.9 0.0 copy-done.11
  18.9 0.0 copy-done.12
  18.9 0.0 copy-done.1
  18.9 2.6 %shard_map.120 = bf16[16,32,256]{2,1,0:T(8,128)(2,1)S(1)} custom-call(s32[16]{0:T(128)S(1)} %copy-done.10, s32[2,1,8]{2,1,0:T(1,128)S(1)} %copy-done.9, bf16[16,2,16,128]{3,2,1,0:T(8,128)(2,1)S(1)} %copy-done.1, bf16[16,2,16,128]{3,2,1,0:T(8,128)(2,1)S(1)} %collective-permute-done.up_ref, bf16[16,2,16,128]{3,2,1,0:T(8,128)(2,1)S(1)} %collective-permute-done.1.down_ref, ...), custom_call_target="tpu_custom_call" | custom-call | flops 1000000000 | bytes 1000000 | tf_op jit(solution)/shard_map/pallas_call | solution.py:291
  21.5 0.0 copy-start.2
  21.5 0.0 copy-start.4
  21.5 21.6 %all_to_all.5.parts_ref = bf16[16,32,256]{2,1,0:T(8,128)(2,1)S(1)} all-to-all(bf16[16,32,256]{2,1,0:T(8,128)(2,1)S(1)} %shard_map.120), channel_id=1, replica_groups=mesh['tm'=16,'row'=8,'col'=4] {'tm'}, dimensions={0} | all-to-all | bytes 524288 | tf_op jit(solution)/shard_map/all_to_all | solution.py:317
  43.1 0.0 copy-done.2
  43.1 0.0 copy-done.4
  43.1 1.3 %shard_map.121 = f32[8,1024]{1,0:T(8,128)} custom-call(bf16[16,32,256]{2,1,0:T(8,128)(2,1)S(1)} %all_to_all.5.parts_ref, f32[64,32]{1,0:T(8,128)S(1)} %copy-done.4, f32[256,32]{1,0:T(8,128)S(1)} %copy-done.2), custom_call_target="tpu_custom_call" | custom-call | flops 100000000 | bytes 1000000 | tf_op jit(solution)/shard_map/pallas_call | solution.py:318
Async XLA Ops:
  0.0 6.5 %collective-permute-start.1 = (bf16[16,2,16,128]{3,2,1,0:T(8,128)(2,1)}, bf16[16,2,16,128]{3,2,1,0:T(8,128)(2,1)S(1)}, u32[]{:S(2)}, u32[]{:S(2)}) collective-permute-start(bf16[16,2,16,128]{3,2,1,0:T(8,128)(2,1)} %own_ref.3), channel_id=1, source_target_pairs={{4,0},{8,4},{12,8},{16,12},{20,16},{24,20},{28,24},{5,1},{9,5},{13... | collective-permute-start | bytes 393224 | tf_op jit(solution)/shard_map/ppermute | solution.py:245
  1.9 7.7 %collective-permute-start = (bf16[16,2,16,128]{3,2,1,0:T(8,128)(2,1)}, bf16[16,2,16,128]{3,2,1,0:T(8,128)(2,1)S(1)}, u32[]{:S(2)}, u32[]{:S(2)}) collective-permute-start(bf16[16,2,16,128]{3,2,1,0:T(8,128)(2,1)} %own_ref.3), channel_id=1, source_target_pairs={{0,4},{4,8},{8,12},{12,16},{16,20},{20,24},{24,28},{1,5},{5,9},{9,... | collective-permute-start | bytes 393224 | tf_op jit(solution)/shard_map/ppermute | solution.py:245
  9.6 0.9 %copy-start = (bf16[16,2,16,128]{3,2,1,0:T(8,128)(2,1)S(1)}, bf16[16,2,16,128]{3,2,1,0:T(8,128)(2,1)}, u32[]{:S(2)}) copy-start(bf16[16,2,16,128]{3,2,1,0:T(8,128)(2,1)} %own_ref.3) | copy-start | bytes 393220
  10.5 5.7 %copy-start.3 = (bf16[256,32]{1,0:T(8,128)(2,1)S(1)}, bf16[256,32]{1,0:T(8,128)(2,1)}, u32[]{:S(2)}) copy-start(bf16[256,32]{1,0:T(8,128)(2,1)} %constant.15.clone.table_ref) | copy-start | bytes 49156
  10.5 5.7 %copy-start.5 = (bf16[36,192]{1,0:T(8,128)(2,1)S(1)}, bf16[36,192]{1,0:T(8,128)(2,1)}, u32[]{:S(2)}) copy-start(bf16[36,192]{1,0:T(8,128)(2,1)} %constant.16.clone.spread_ref) | copy-start | bytes 41476
  10.5 5.7 %copy-start.6 = (bf16[32,256]{1,0:T(8,128)(2,1)S(1)}, bf16[32,256]{1,0:T(8,128)(2,1)}, u32[]{:S(2)}) copy-start(bf16[32,256]{1,0:T(8,128)(2,1)} %constant.14.clone.packed_ref) | copy-start | bytes 49156
  10.5 5.8 %copy-start.7 = (bf16[32,36]{1,0:T(8,128)(2,1)S(1)}, bf16[32,36]{1,0:T(8,128)(2,1)}, u32[]{:S(2)}) copy-start(bf16[32,36]{1,0:T(8,128)(2,1)} %rows_ref.2) | copy-start | bytes 6916
  10.5 5.8 %copy-start.8 = (bf16[32,36]{1,0:T(8,128)(2,1)S(1)}, bf16[32,36]{1,0:T(8,128)(2,1)}, u32[]{:S(2)}) copy-start(bf16[32,36]{1,0:T(8,128)(2,1)} %cols_ref.1) | copy-start | bytes 6916
  10.5 5.8 %copy-start.9 = (s32[2,1,8]{2,1,0:T(1,128)S(1)}, s32[2,1,8]{2,1,0:T(1,128)}, u32[]{:S(2)}) copy-start(s32[2,1,8]{2,1,0:T(1,128)} %shift_ref.3) | copy-start | bytes 196
  10.6 8.4 %copy-start.10 = (s32[16]{0:T(128)S(1)}, s32[16]{0:T(128)}, u32[]{:S(2)}) copy-start(s32[16]{0:T(128)} %phase_ref.1) | copy-start | bytes 196
  10.6 8.4 %copy-start.11 = (bf16[160,256]{1,0:T(8,128)(2,1)S(1)}, bf16[160,256]{1,0:T(8,128)(2,1)}, u32[]{:S(2)}) copy-start(bf16[160,256]{1,0:T(8,128)(2,1)} %constant.17.clone.first_ref) | copy-start | bytes 245764
  10.6 8.3 %copy-start.12 = (bf16[256,128]{1,0:T(8,128)(2,1)S(1)}, bf16[256,128]{1,0:T(8,128)(2,1)}, u32[]{:S(2)}) copy-start(bf16[256,128]{1,0:T(8,128)(2,1)} %constant.18.clone.left_ref) | copy-start | bytes 196612
  10.8 8.1 %copy-start.1 = (bf16[16,2,16,128]{3,2,1,0:T(8,128)(2,1)S(1)}, bf16[16,2,16,128]{3,2,1,0:T(8,128)(2,1)}, u32[]{:S(2)}) copy-start(bf16[16,2,16,128]{3,2,1,0:T(8,128)(2,1)} %own_ref.3) | copy-start | bytes 393220
  10.8 6.4 %collective-permute-start.2 = (bf16[16,1536]{1,0:T(8,128)(2,1)S(1)}, bf16[16,1536]{1,0:T(8,128)(2,1)S(1)}, u32[]{:S(2)}, u32[]{:S(2)}) collective-permute-start(bf16[16,1536]{1,0:T(8,128)(2,1)S(1)} %get-tuple-element.11), channel_id=1, source_target_pairs={{0,1},{1,2},{2,3},{4,5},{5,6},{6,7},{8,9},{9,10},{10,11},{12,13},{... | collective-permute-start | bytes 147464 | tf_op jit(solution)/shard_map/ppermute | solution.py:245
  14.1 4.8 %collective-permute-start.3 = (bf16[16,1536]{1,0:T(8,128)(2,1)S(1)}, bf16[16,1536]{1,0:T(8,128)(2,1)S(1)}, u32[]{:S(2)}, u32[]{:S(2)}) collective-permute-start(bf16[16,1536]{1,0:T(8,128)(2,1)S(1)} %get-tuple-element.12), channel_id=1, source_target_pairs={{1,0},{2,1},{3,2},{5,4},{6,5},{7,6},{9,8},{10,9},{11,10},{13,12},{... | collective-permute-start | bytes 147464 | tf_op jit(solution)/shard_map/ppermute | solution.py:245
  21.5 21.6 %copy-start.2 = (f32[256,32]{1,0:T(8,128)S(1)}, f32[256,32]{1,0:T(8,128)}, u32[]{:S(2)}) copy-start(f32[256,32]{1,0:T(8,128)} %constant.20.clone.places_ref) | copy-start | bytes 98308
  21.5 21.6 %copy-start.4 = (f32[64,32]{1,0:T(8,128)S(1)}, f32[64,32]{1,0:T(8,128)}, u32[]{:S(2)}) copy-start(f32[64,32]{1,0:T(8,128)} %constant.19.clone.rows_ref) | copy-start | bytes 24580

commit v3 on v2

v3 whole, which is shorter than its diff:
```python
import math
from functools import partial

import jax
import jax.numpy as jnp
import numpy as np
from jax import lax
from jax.experimental import pallas as pl
from jax.experimental.pallas import tpu as pltpu
from jax.sharding import PartitionSpec as P

WIN = 32
STEP = 16
BAND = 2
HALO = 16
SLOTS = WIN // 2
PATCH = WIN + 2 * BAND
SPAN = 40
GROUP = 4
QUARTERS = 4

F32 = jnp.float32
BF16 = jnp.bfloat16
HIGHEST = lax.Precision.HIGHEST


def dot(a, b, dims=((1,), (0,)), precision=None):
    return lax.dot_general(a, b, (dims, ((), ())), precision=precision, preferred_element_type=F32)


def tables():
    index = np.arange(WIN)
    angles = (index[:, None] * index[None, :] % WIN).astype(np.float32) * np.float32(2.0 * math.pi / WIN)
    return np.cos(angles).astype(np.float32), np.sin(angles).astype(np.float32)


def as_bf16(values):
    return np.asarray(values, np.float32).astype(jnp.bfloat16)


def constants(windows):
    cosine, sine = tables()
    cos_half = as_bf16(cosine).astype(np.float32)
    sin_half = as_bf16(sine).astype(np.float32)
    real = cos_half[:, :SLOTS]
    imag = -sin_half[:, :SLOTS]
    imag[:, 0] = cos_half[:, SLOTS]
    packed = np.concatenate([np.tile(real, (1, windows)), np.tile(imag, (1, windows))], axis=1)
    lanes = windows * SLOTS
    first = np.zeros((2 * HALO + windows * STEP, 2 * lanes), np.float32)
    for w in range(windows):
        top = HALO - (WIN - STEP) // 2 + STEP * w
        first[top : top + WIN, w * SLOTS : (w + 1) * SLOTS] = real
        first[top : top + WIN, lanes + w * SLOTS : lanes + (w + 1) * SLOTS] = imag
    own = first[HALO : HALO + windows * STEP]
    order = np.concatenate([own, first[:HALO], first[HALO + windows * STEP :]], axis=0)
    edges = np.zeros((QUARTERS,) + order.shape, np.float32)
    for h in range(QUARTERS):
        for half in range(2):
            for at, w in enumerate((0, windows - 1)):
                to = half * lanes + (2 * h + at) * SLOTS
                of = half * lanes + w * SLOTS
                edges[h, :, to : to + SLOTS] = order[:, of : of + SLOTS]
    rows = np.concatenate([np.tile(cos_half, (GROUP, 1)), np.tile(sin_half, (GROUP, 1))], axis=0)
    block = np.tile(np.repeat(np.arange(GROUP), WIN), 2)
    left_a = np.where(block[:, None] == np.repeat(np.arange(GROUP), WIN)[None, :], np.tile(rows, (1, GROUP)), 0.0)
    lag = np.arange(WIN)
    back_real = 2.0 * cosine[:SLOTS]
    back_imag = -2.0 * sine[:SLOTS]
    back_real[0] = 1.0
    back_imag[0] = np.where(lag % 2 == 0, 1.0, -1.0)
    folded = np.concatenate([np.tile(back_real, (windows, 1)), np.tile(back_imag, (windows, 1))], axis=0) / WIN**3
    inverse_rows = np.concatenate([cosine, sine], axis=0)
    return dict(
        table=as_bf16(np.concatenate([packed, rows.T], axis=1)),
        own=as_bf16(own),
        edges=as_bf16(edges),
        left_a=as_bf16(left_a),
        places=folded,
        inverse_rows=inverse_rows,
    )


def whole(space=pltpu.VMEM):
    return pl.BlockSpec(memory_space=space)


def take_strips(ref, right_ref, left_ref, start):
    pairs, _, tile_rows, tile_cols = ref.shape
    row = lax.broadcasted_iota(jnp.int32, (2 * HALO, tile_cols), 0)
    col = lax.broadcasted_iota(jnp.int32, (2 * HALO, tile_cols), 1)
    wanted = jnp.where(row < HALO, row + (tile_cols - HALO), row - HALO)
    pick = (col == wanted).astype(F32).astype(BF16)
    span = pairs * tile_rows
    for image in range(2):
        pixels = ref[:, image].reshape(span, tile_cols)
        taken = dot(pick, pixels, ((1,), (1,))).astype(BF16)
        place = slice(start + image * span, start + (image + 1) * span)
        right_ref[:, place] = taken[:HALO]
        left_ref[:, place] = taken[HALO:]


def strips_kernel(up_ref, own_right_ref, own_left_ref, down_ref, right_ref, left_ref):
    width = own_right_ref.shape[1]
    take_strips(up_ref, right_ref, left_ref, 0)
    right_ref[:, width : 2 * width] = own_right_ref[...]
    left_ref[:, width : 2 * width] = own_left_ref[...]
    take_strips(down_ref, right_ref, left_ref, 2 * width)


def fetch(sources, targets, sems):
    copies = [pltpu.make_async_copy(a, b, sems.at[i]) for i, (a, b) in enumerate(zip(sources, targets))]
    for copy in copies:
        copy.start()
    return copies


def weights_kernel(
    shift_hbm,
    phase_hbm,
    frames_hbm,
    rows_hbm,
    cols_hbm,
    table_hbm,
    moved_ref,
    bins_ref,
    own_ref,
    high_ref,
    low_ref,
    ehigh_ref,
    elow_ref,
    rhigh_ref,
    rlow_ref,
    right_ref,
    left_ref,
    shift_ref,
    rows_ref,
    cols_ref,
    table_ref,
    wide_ref,
    sems,
):
    copies = fetch(
        (shift_hbm, rows_hbm, cols_hbm, table_hbm, shift_hbm, phase_hbm, frames_hbm),
        (shift_ref, rows_ref, cols_ref, table_ref, moved_ref, bins_ref, own_ref),
        sems,
    )
    windows = shift_ref.shape[2]
    lanes = wide_ref.shape[2]
    for copy in copies[:4]:
        copy.wait()
    packed, turned = table_ref[:, : 2 * lanes], table_ref[:, 2 * lanes :]
    column = dot(cols_ref[...], packed, ((0,), (0,)))
    column = jnp.concatenate([column, jnp.zeros((40 - PATCH, 2 * lanes), F32)], axis=0)
    wide_ref[...] = jnp.zeros_like(wide_ref)
    owner = lax.broadcasted_iota(jnp.int32, (40, lanes), 1) // SLOTS
    for w in range(windows):
        start = STEP * w + HALO - (WIN - STEP) // 2 - BAND + shift_ref[1, 0, w]
        rows = pl.ds(start, 40)
        for t in range(2):
            wide_ref[t, rows, :] = jnp.where(
                owner == w, column[:, t * lanes : (t + 1) * lanes], wide_ref[t, rows, :]
            )
    inner = slice(HALO, HALO + high_ref.shape[0])
    right = slice(inner.stop, inner.stop + HALO)
    lane = lax.broadcasted_iota(jnp.int32, (1, lanes), 1)
    for t in range(2):
        place = slice(t * lanes, (t + 1) * lanes)
        values = wide_ref[t, inner, :]
        high = values.astype(BF16)
        high_ref[:, place] = high
        low_ref[:, place] = (values - high.astype(F32)).astype(BF16)
        values = jnp.concatenate([values, wide_ref[t, :HALO, :], wide_ref[t, right, :]], axis=0)
        ends = jnp.where(lane < SLOTS, values, 0.0) + jnp.where(
            lane // SLOTS == 1, pltpu.roll(values, 2 * SLOTS, 1), 0.0
        )
        for h in range(QUARTERS):
            placed = ends if h == 0 else pltpu.roll(ends, 2 * SLOTS * h, 1)
            high = placed.astype(BF16)
            ehigh_ref[h, :, place] = high
            elow_ref[h, :, place] = (placed - high.astype(F32)).astype(BF16)
    place = lax.broadcasted_iota(jnp.int32, (PATCH, GROUP * SPAN), 1) % SPAN
    spread = (place == lax.broadcasted_iota(jnp.int32, (PATCH, GROUP * SPAN), 0)).astype(F32).astype(BF16)
    spread = dot(rows_ref[...], spread).astype(BF16)
    left = dot(turned, spread, ((0,), (0,)))
    mine = (lax.broadcasted_iota(jnp.int32, left.shape, 0) // WIN) % GROUP
    theirs = lax.broadcasted_iota(jnp.int32, left.shape, 1) // SPAN
    left = jnp.where(mine == theirs, left, 0.0)
    high = left.astype(BF16)
    rhigh_ref[...] = high
    rlow_ref[...] = (left - high.astype(F32)).astype(BF16)
    for copy in copies[4:]:
        copy.wait()
    take_strips(own_ref, right_ref, left_ref, 0)


def starts(shift_ref, windows):
    return [HALO - (WIN - STEP) // 2 - BAND + shift_ref[0, 0, w] for w in windows]


def cross_spectra(half_a, half_b, pairs, offsets, owner, left_ref, rhigh_ref, rlow_ref):
    lanes = half_b.shape[3]
    head = (half_a.shape[1] - WIN) // 2
    zero_slot = lax.broadcasted_iota(jnp.int32, (1, lanes), 1) % SLOTS == 0
    first_row = lax.broadcasted_iota(jnp.int32, (GROUP * WIN, 1), 0) % WIN == 0
    part_a, part_b = [], []
    for p in pairs:
        real = half_a[p, head : head + WIN, :lanes]
        mean = jnp.sum(real, axis=0, keepdims=True) * (1.0 / WIN)
        real = real - jnp.where(zero_slot, mean, 0.0)
        part_a.append(jnp.concatenate([real, half_a[p, head : head + WIN, lanes:]], axis=1))
        lined = []
        for t in range(2):
            taken = half_b[t, p, pl.ds(offsets[0], SPAN), :]
            for w in range(1, len(offsets)):
                taken = jnp.where(owner == w, half_b[t, p, pl.ds(offsets[w], SPAN), :], taken)
            lined.append(taken)
        part_b.append(jnp.concatenate(lined, axis=1))
    rows_a = jnp.concatenate(part_a, axis=0).astype(BF16)
    rows_b = jnp.concatenate(part_b, axis=0)
    high = rows_b.astype(BF16)
    low = (rows_b - high.astype(F32)).astype(BF16)
    spec_a = dot(left_ref[...], rows_a)
    spec_b = dot(rhigh_ref[...], high) + dot(rhigh_ref[...], low) + dot(rlow_ref[...], high)
    half_rows = GROUP * WIN
    a_cr, a_ci = spec_a[:half_rows, :lanes], spec_a[:half_rows, lanes:]
    a_sr, a_si = spec_a[half_rows:, :lanes], spec_a[half_rows:, lanes:]
    b_cr, b_ci = spec_b[:half_rows, :lanes], spec_b[:half_rows, lanes:]
    b_sr, b_si = spec_b[half_rows:, :lanes], spec_b[half_rows:, lanes:]
    b_cr = jnp.where(zero_slot & first_row, 0.0, b_cr)
    a_real, a_imag = a_cr + jnp.where(zero_slot, 0.0, a_si), jnp.where(zero_slot, 0.0, a_ci) - a_sr
    b_real, b_imag = b_cr + jnp.where(zero_slot, 0.0, b_si), jnp.where(zero_slot, 0.0, b_ci) - b_sr
    last_real = jnp.where(zero_slot, a_ci * b_ci + a_si * b_si, 0.0)
    last_imag = jnp.where(zero_slot, a_si * b_ci - a_ci * b_si, 0.0)
    cross_real = a_real * b_real + a_imag * b_imag - last_imag
    cross_imag = a_real * b_imag - a_imag * b_real + last_real
    return cross_real, cross_imag


def inner_kernel(
    phase_vec,
    shift_vec,
    own_ref,
    up_ref,
    down_ref,
    first_ref,
    high_ref,
    low_ref,
    left_ref,
    rhigh_ref,
    rlow_ref,
    sums,
    half_a,
    half_b,
    phase_ref,
    shift_ref,
    sems,
):
    copies = fetch((phase_vec, shift_vec), (phase_ref, shift_ref), sems)
    pairs, _, tile_rows, tile_cols = own_ref.shape
    windows = shift_ref.shape[2]
    lanes = windows * SLOTS
    span = pairs * tile_rows
    for at, ref in enumerate((up_ref, own_ref, down_ref)):
        rows = slice(at * tile_rows, (at + 1) * tile_rows)
        pixels = ref[:, 0].reshape(span, tile_cols)
        half_a[:, rows, :] = dot(pixels, first_ref[...]).reshape(pairs, tile_rows, 2 * lanes)
        pixels = ref[:, 1].reshape(span, tile_cols)
        half = dot(pixels, high_ref[...]) + dot(pixels, low_ref[...])
        for t in range(2):
            half_b[t, :, rows, :] = half[:, t * lanes : (t + 1) * lanes].reshape(pairs, tile_rows, lanes)
    half_b[:, :, 3 * tile_rows :, :] = jnp.zeros((2, pairs, half_b.shape[2] - 3 * tile_rows, lanes), F32)
    sums[...] = jnp.zeros_like(sums)
    owner = lax.broadcasted_iota(jnp.int32, (1, lanes), 1) // SLOTS
    for copy in copies:
        copy.wait()
    offsets = starts(shift_ref, range(windows))
    for g in range(pairs // GROUP):
        members = range(g * GROUP, (g + 1) * GROUP)
        real, imag = cross_spectra(half_a, half_b, members, offsets, owner, left_ref, rhigh_ref, rlow_ref)
        for q, p in enumerate(members):
            b = phase_ref[p]
            rows = slice(q * WIN, (q + 1) * WIN)
            sums[b, :, :lanes] += real[rows]
            sums[b, :, lanes:] += imag[rows]


def edge_kernel(
    phase_vec,
    shift_vec,
    own_ref,
    up_ref,
    down_ref,
    before_ref,
    after_ref,
    first_ref,
    high_ref,
    low_ref,
    left_ref,
    rhigh_ref,
    rlow_ref,
    inner_ref,
    out_ref,
    half_a,
    half_b,
    sums,
    phase_ref,
    shift_ref,
    sems,
):
    copies = fetch((phase_vec, shift_vec), (phase_ref, shift_ref), sems)
    pairs, _, tile_rows, tile_cols = own_ref.shape
    windows = shift_ref.shape[2]
    lanes = windows * SLOTS
    span = pairs * tile_rows
    part = span // QUARTERS
    each = pairs // QUARTERS

    def along_columns(pixels, weights_ref):
        total = dot(pixels[:part], weights_ref[0])
        for h in range(1, QUARTERS):
            total = total + dot(pixels[h * part : (h + 1) * part], weights_ref[h])
        return total

    for at, ref in enumerate((up_ref, own_ref, down_ref)):
        rows = slice(at * tile_rows, (at + 1) * tile_rows)
        taken = []
        for image in range(2):
            place = slice((2 * at + image) * span, (2 * at + image + 1) * span)
            strip = jnp.concatenate([before_ref[:, place], after_ref[:, place]], axis=0)
            strip = jnp.transpose(strip.astype(F32)).astype(BF16)
            taken.append(jnp.concatenate([ref[:, image].reshape(span, tile_cols), strip], axis=1))
        half_a[:, rows, :] = along_columns(taken[0], first_ref).reshape(each, tile_rows, 2 * lanes)
        half = along_columns(taken[1], high_ref) + along_columns(taken[1], low_ref)
        for t in range(2):
            half_b[t, :, rows, :] = half[:, t * lanes : (t + 1) * lanes].reshape(each, tile_rows, lanes)
    half_b[:, :, 3 * tile_rows :, :] = jnp.zeros((2, each, half_b.shape[2] - 3 * tile_rows, lanes), F32)
    sums[...] = jnp.zeros_like(sums)
    lane = lax.broadcasted_iota(jnp.int32, (1, lanes), 1)
    for copy in copies:
        copy.wait()
    offsets = starts(shift_ref, (0, windows - 1))
    real, imag = cross_spectra(
        half_a, half_b, range(each), offsets, (lane // SLOTS) % 2, left_ref, rhigh_ref, rlow_ref
    )
    for q in range(each):
        rows = slice(q * WIN, (q + 1) * WIN)
        for h in range(QUARTERS):
            b = phase_ref[h * each + q]
            mine = lane // (2 * SLOTS) == h
            sums[b, :, :lanes] += jnp.where(mine, real[rows], 0.0)
            sums[b, :, lanes:] += jnp.where(mine, imag[rows], 0.0)
    edge = (lane < SLOTS) | (lane >= lanes - SLOTS)
    for b in range(sums.shape[0]):
        for t in range(2):
            place = slice(t * lanes, (t + 1) * lanes)
            total = sums[b, :, place]
            total = total + pltpu.roll(total, lanes // 2, 1)
            total = total + pltpu.roll(total, lanes // 4, 1)
            out_ref[b, :, place] = jnp.where(edge, total, inner_ref[b, :, place]).astype(BF16)


def inverse_kernel(parts_ref, rows_ref, places_ref, out_ref, lines):
    windows = out_ref.shape[0]
    lanes = windows * SLOTS
    total = jnp.sum(parts_ref[...].astype(F32), axis=0)
    turned = dot(rows_ref[...], total, precision=HIGHEST)
    lines[:, :lanes] = turned[:WIN, :lanes] - turned[WIN:, lanes:]
    lines[:, lanes:] = turned[WIN:, :lanes] + turned[:WIN, lanes:]
    owner = (lax.broadcasted_iota(jnp.int32, (windows, 2 * lanes), 1) % lanes) // SLOTS
    own = owner == lax.broadcasted_iota(jnp.int32, (windows, 2 * lanes), 0)
    spread = jnp.concatenate(
        [jnp.where(own, jnp.broadcast_to(lines[u : u + 1, :], (windows, 2 * lanes)), 0.0) for u in range(WIN)],
        axis=0,
    )
    planes = dot(spread, places_ref[...], precision=HIGHEST)
    for u in range(WIN):
        out_ref[:, u * WIN : (u + 1) * WIN] = planes[u * windows : (u + 1) * windows]


def shifted(values, axis, step):
    count = lax.axis_size(axis)
    return lax.ppermute(values, axis, [(i, i + step) for i in range(count) if 0 <= i + step < count])


def stay(*values):
    return [pltpu.with_memory_space_constraint(jnp.asarray(value), pltpu.HBM) for value in values]


def call(kernel, outs, specs, scratch=(), flops=0, size=0, room=16):
    return pl.pallas_call(
        kernel,
        out_shape=outs,
        in_specs=specs,
        out_specs=jax.tree.map(lambda _: whole(), outs),
        scratch_shapes=scratch,
        compiler_params=pltpu.CompilerParams(vmem_limit_bytes=room << 20),
        cost_estimate=pl.CostEstimate(flops=flops, bytes_accessed=size, transcendentals=0),
    )


def body(frames, phase, shift, interp_rows, interp_cols):
    pairs, _, tile_rows, tile_cols = frames.shape
    windows = tile_cols // STEP
    lanes = windows * SLOTS
    bins = lax.axis_size("tm")
    fixed = constants(windows)
    shape = jax.ShapeDtypeStruct
    vmem, hbm = whole(), whole(pltpu.HBM)

    up = shifted(frames, "row", 1)
    down = shifted(frames, "row", -1)
    wide = 2 * HALO + tile_cols
    strip = shape((HALO, 2 * pairs * tile_rows), BF16)
    scalars = pltpu.SMEM(shift.shape, shift.dtype)
    weights = shape((tile_cols, 2 * lanes), BF16)
    ends = shape((QUARTERS, wide, 2 * lanes), BF16)
    left = shape((2 * GROUP * WIN, GROUP * SPAN), BF16)
    moved, phases, own, high, low, ehigh, elow, rhigh, rlow, own_right, own_left = call(
        weights_kernel,
        (
            shape(shift.shape, shift.dtype),
            shape(phase.shape, phase.dtype),
            shape(frames.shape, BF16),
            weights,
            weights,
            ends,
            ends,
            left,
            left,
            strip,
            strip,
        ),
        [hbm] * 6,
        scratch=[
            scalars,
            pltpu.VMEM(interp_rows.shape, BF16),
            pltpu.VMEM(interp_cols.shape, BF16),
            pltpu.VMEM(fixed["table"].shape, BF16),
            pltpu.VMEM((2, wide + 8, lanes), F32),
            pltpu.SemaphoreType.DMA((7,)),
        ],
        flops=10**7,
        size=400000,
    )(*stay(shift, phase, frames, interp_rows, interp_cols, fixed["table"]))

    side = shape((HALO, 6 * pairs * tile_rows), BF16)
    rightward, leftward = call(strips_kernel, (side, side), [vmem] * 4, flops=10**7, size=200000)(
        up, own_right, own_left, down
    )
    before = shifted(rightward, "col", 1)
    after = shifted(leftward, "col", -1)

    tall = 3 * tile_rows
    fetched = [pltpu.SMEM(phase.shape, phase.dtype), scalars, pltpu.SemaphoreType.DMA((2,))]
    inner = call(
        inner_kernel,
        shape((bins, WIN, 2 * lanes), F32),
        [vmem] * 11,
        scratch=[pltpu.VMEM((pairs, tall, 2 * lanes), F32), pltpu.VMEM((2, pairs, tall + 8, lanes), F32)] + fetched,
        flops=10**9,
        size=10**6,
    )(phases, moved, own, up, down, fixed["own"], high, low, fixed["left_a"], rhigh, rlow)
    each = pairs // QUARTERS
    partial_sums = call(
        edge_kernel,
        shape((bins, WIN, 2 * lanes), BF16),
        [vmem] * 14,
        scratch=[
            pltpu.VMEM((each, tall, 2 * lanes), F32),
            pltpu.VMEM((2, each, tall + 8, lanes), F32),
            pltpu.VMEM((bins, WIN, 2 * lanes), F32),
        ]
        + fetched,
        flops=10**9,
        size=10**6,
    )(
        phases,
        moved,
        own,
        up,
        down,
        before,
        after,
        fixed["edges"],
        ehigh,
        elow,
        fixed["left_a"],
        rhigh,
        rlow,
        inner,
    )
    parts = lax.all_to_all(partial_sums, "tm", 0, 0, tiled=True)
    planes = call(
        inverse_kernel,
        shape((windows, WIN * WIN), F32),
        [vmem] * 3,
        scratch=[pltpu.VMEM((WIN, 2 * lanes), F32)],
        flops=10**8,
        size=10**6,
    )(parts, fixed["inverse_rows"], fixed["places"])
    return planes[None, None]


def solution(mesh):
    placed = (P("tm", None, "row", "col"), P("tm"), P(None, "row", "col"), P(), P())
    return jax.shard_map(
        body, mesh=mesh, in_specs=placed, out_specs=P("tm", "row", "col", None), check_vma=False
    )
```

time: 44.7 us -> 42.5 us (0.951)
  waiting for transfers between devices: 6 us -> 3.66 us
  Pallas kernels: 5.01 us -> 6.32 us
  local copies, waits for them, and re-layouts: 0.97 us -> 0.03 us
    ppermute x4, waiting for transfers between devices: 6 us -> 3.66 us  [shifted(): lax.ppermute(values, axis, [(i, i + step) for i in range(count) if 0 <= i...]
    pallas_call x3 -> x4, Pallas kernels: 3.67 us -> 4.98 us  [the longest x1 1.7 us: body(): call(inner_kernel, shape((bins, WIN, 2 * lanes), F32), [vmem] * 11, scrat...]
    unnamed x26 -> x10, local copies, waits for them, and re-layouts: 0.97 us -> 0.03 us
  transfers between devices with their start and end apart: 4 -> 4, of which waited for: 3 -> 2; matrix products, arithmetic and copies ran while one was open for 0% -> 0% of each run, Pallas kernels for 2% -> 8%
where the time goes in v3:
time: 42.5 us; the launch traced here: 42.3 us
  blocking collectives  21.6 us (51%)
  starting transfers between devices  10.6 us (25%)
  Pallas kernels  6.32 us (15%)
  waiting for transfers between devices  3.66 us (9%)
    all_to_all x1, blocking collectives, body(): parts = lax.all_to_all(partial_sums, 'tm', 0, 0, tiled=True)  21.6 us
    ppermute x4, starting transfers between devices, shifted(): lax.ppermute(values, axis, [(i, i + step) for i in range(count) if 0 <= i...  10.6 us
    ppermute x4, waiting for transfers between devices, shifted(): lax.ppermute(values, axis, [(i, i + step) for i in range(count) if 0 <= i...  3.66 us
    pallas_call x1, Pallas kernels, body(): call(inner_kernel, shape((bins, WIN, 2 * lanes), F32), [vmem] * 11, scrat...  1.7 us
    pallas_call x1, Pallas kernels, body(): call(weights_kernel, (shape(shift.shape, shift.dtype), shape(phase.shape,...  1.57 us
    pallas_call x1, Pallas kernels, body(): call(edge_kernel, shape((bins, WIN, 2 * lanes), BF16), [vmem] * 14, scrat...  1.55 us
    pallas_call x1, Pallas kernels, body(): call(inverse_kernel, shape((windows, WIN * WIN), F32), [vmem] * 3, scratc...  1.34 us
  transfers between devices with their start and end apart: 4, of which 2 were waited for; matrix products, arithmetic and copies ran while one was open for 0% of the time, Pallas kernels for 8%

profile of v3, /device:TPU:259, one launch (start us, length us, event | category | flops | bytes accessed | tf_op | source)
XLA Modules:
  0.0 42.3 jit_solution(8337507772101879724)
XLA Ops:
  0.0 1.9 %collective-permute-start.1 = (bf16[16,2,16,128]{3,2,1,0:T(8,128)(2,1)}, bf16[16,2,16,128]{3,2,1,0:T(8,128)(2,1)S(1)}, u32[]{:S(2)}, u32[]{:S(2)}) collective-permute-start(bf16[16,2,16,128]{3,2,1,0:T(8,128)(2,1)} %frames_hbm.1), channel_id=1, source_target_pairs={{4,0},{8,4},{12,8},{16,12},{20,16},{24,20},{28,24},{5,1},{9,5},{13... | collective-permute-start | bytes 393224 | tf_op jit(solution)/shard_map/ppermute | solution.py:383
  1.9 3.4 %collective-permute-start = (bf16[16,2,16,128]{3,2,1,0:T(8,128)(2,1)}, bf16[16,2,16,128]{3,2,1,0:T(8,128)(2,1)S(1)}, u32[]{:S(2)}, u32[]{:S(2)}) collective-permute-start(bf16[16,2,16,128]{3,2,1,0:T(8,128)(2,1)} %frames_hbm.1), channel_id=1, source_target_pairs={{0,4},{4,8},{8,12},{12,16},{16,20},{20,24},{24,28},{1,5},{5,9},{9,... | collective-permute-start | bytes 393224 | tf_op jit(solution)/shard_map/ppermute | solution.py:383
  5.3 1.6 %shard_map.109 = (s32[2,1,8]{2,1,0:T(1,128)S(1)}, s32[16]{0:T(128)S(1)}, bf16[16,2,16,128]{3,2,1,0:T(8,128)(2,1)S(1)}, bf16[128,256]{1,0:T(8,128)(2,1)S(1)}, bf1...) custom-call(s32[2,1,8]{2,1,0:T(1,128)} %shift_hbm.1, ...), custom_call_target="tpu_custom_call" | custom-call | flops 10000000 | bytes 400000 | tf_op jit(solution)/shard_map/pallas_call | solution.py:419
  6.9 0.0 collective-permute-done.1.down_ref
  6.9 2.7 %collective-permute-done.up_ref = bf16[16,2,16,128]{3,2,1,0:T(8,128)(2,1)S(1)} collective-permute-done((bf16[16,2,16,128]{3,2,1,0:T(8,128)(2,1)}, bf16[16,2,16,128]{3,2,1,0:T(8,128)(2,1)S(1)}, u32[]{:S(2)}, u32[]{:S(2)}) %collective-permute-start) | collective-permute-done | bytes 131104 | tf_op jit(solution)/shard_map/ppermute | solution.py:383
  9.6 0.0 copy-start.3
  9.6 0.0 copy-start.4
  9.6 0.2 shard_map.110
  9.8 3.1 %collective-permute-start.2 = (bf16[16,1536]{1,0:T(8,128)(2,1)S(1)}, bf16[16,1536]{1,0:T(8,128)(2,1)S(1)}, u32[]{:S(2)}, u32[]{:S(2)}) collective-permute-start(bf16[16,1536]{1,0:T(8,128)(2,1)S(1)} %get-tuple-element.23), channel_id=1, source_target_pairs={{0,1},{1,2},{2,3},{4,5},{5,6},{6,7},{8,9},{9,10},{10,11},{12,13},{... | collective-permute-start | bytes 147464 | tf_op jit(solution)/shard_map/ppermute | solution.py:383
  12.9 2.2 %collective-permute-start.3 = (bf16[16,1536]{1,0:T(8,128)(2,1)S(1)}, bf16[16,1536]{1,0:T(8,128)(2,1)S(1)}, u32[]{:S(2)}, u32[]{:S(2)}) collective-permute-start(bf16[16,1536]{1,0:T(8,128)(2,1)S(1)} %get-tuple-element.24), channel_id=1, source_target_pairs={{1,0},{2,1},{3,2},{5,4},{6,5},{7,6},{9,8},{10,9},{11,10},{13,12},{... | collective-permute-start | bytes 147464 | tf_op jit(solution)/shard_map/ppermute | solution.py:383
  15.1 0.0 copy-done.3
  15.1 0.0 copy-done.4
  15.1 0.0 copy-start.2
  15.1 1.7 %shard_map.111.inner_ref = f32[16,32,256]{2,1,0:T(8,128)S(1)} custom-call(s32[16]{0:T(128)S(1)} %get-tuple-element.18.phase_vec, s32[2,1,8]{2,1,0:T(1,128)S(1)} %get-tuple-element.19.shift_vec, bf16[16,2,16,128]{3,2,1,0:T(8,128)(2,1)S(1)} %get-tuple-element.20.own_ref, bf16[16,2,16,128]{3,2,1,0:T(8,128)(2,1)S(1)} %collective-permute-done.up_ref, ...), custom_call_target="tpu_custom_call" | custom-call | flops 1000000000 | bytes 1000000 | tf_op jit(solution)/shard_map/pallas_call | solution.py:456
  16.8 0.0 collective-permute-done.2.before_ref
  16.8 0.9 %collective-permute-done.3.after_ref = bf16[16,1536]{1,0:T(8,128)(2,1)S(1)} collective-permute-done((bf16[16,1536]{1,0:T(8,128)(2,1)S(1)}, bf16[16,1536]{1,0:T(8,128)(2,1)S(1)}, u32[]{:S(2)}, u32[]{:S(2)}) %collective-permute-start.3) | collective-permute-done | bytes 49184 | tf_op jit(solution)/shard_map/ppermute | solution.py:383
  17.8 0.0 copy-done.2
  17.8 1.6 %shard_map.112 = bf16[16,32,256]{2,1,0:T(8,128)(2,1)S(1)} custom-call(s32[16]{0:T(128)S(1)} %get-tuple-element.18.phase_vec, s32[2,1,8]{2,1,0:T(1,128)S(1)} %get-tuple-element.19.shift_vec, bf16[16,2,16,128]{3,2,1,0:T(8,128)(2,1)S(1)} %get-tuple-element.20.own_ref, bf16[16,2,16,128]{3,2,1,0:T(8,128)(2,1)S(1)} %collective-permute-done.up_ref, ...), custom_call_target="tpu_custom_call" | custom-call | flops 1000000000 | bytes 1000000 | tf_op jit(solution)/shard_map/pallas_call | solution.py:465
  19.3 0.0 copy-start
  19.3 0.0 copy-start.1
  19.4 21.6 %all_to_all.5.parts_ref = bf16[16,32,256]{2,1,0:T(8,128)(2,1)S(1)} all-to-all(bf16[16,32,256]{2,1,0:T(8,128)(2,1)S(1)} %shard_map.112), channel_id=1, replica_groups=mesh['tm'=16,'row'=8,'col'=4] {'tm'}, dimensions={0} | all-to-all | bytes 524288 | tf_op jit(solution)/shard_map/all_to_all | solution.py:493
  40.9 0.0 copy-done
  40.9 0.0 copy-done.1
  40.9 1.3 %shard_map.113 = f32[8,1024]{1,0:T(8,128)} custom-call(bf16[16,32,256]{2,1,0:T(8,128)(2,1)S(1)} %all_to_all.5.parts_ref, f32[64,32]{1,0:T(8,128)S(1)} %copy-done.1, f32[256,32]{1,0:T(8,128)S(1)} %copy-done), custom_call_target="tpu_custom_call" | custom-call | flops 100000000 | bytes 1000000 | tf_op jit(solution)/shard_map/pallas_call | solution.py:494
Async XLA Ops:
  0.0 6.9 %collective-permute-start.1 = (bf16[16,2,16,128]{3,2,1,0:T(8,128)(2,1)}, bf16[16,2,16,128]{3,2,1,0:T(8,128)(2,1)S(1)}, u32[]{:S(2)}, u32[]{:S(2)}) collective-permute-start(bf16[16,2,16,128]{3,2,1,0:T(8,128)(2,1)} %frames_hbm.1), channel_id=1, source_target_pairs={{4,0},{8,4},{12,8},{16,12},{20,16},{24,20},{28,24},{5,1},{9,5},{13... | collective-permute-start | bytes 393224 | tf_op jit(solution)/shard_map/ppermute | solution.py:383
  1.9 7.7 %collective-permute-start = (bf16[16,2,16,128]{3,2,1,0:T(8,128)(2,1)}, bf16[16,2,16,128]{3,2,1,0:T(8,128)(2,1)S(1)}, u32[]{:S(2)}, u32[]{:S(2)}) collective-permute-start(bf16[16,2,16,128]{3,2,1,0:T(8,128)(2,1)} %frames_hbm.1), channel_id=1, source_target_pairs={{0,4},{4,8},{8,12},{12,16},{16,20},{20,24},{24,28},{1,5},{5,9},{9,... | collective-permute-start | bytes 393224 | tf_op jit(solution)/shard_map/ppermute | solution.py:383
  9.6 5.5 %copy-start.3 = (bf16[256,128]{1,0:T(8,128)(2,1)S(1)}, bf16[256,128]{1,0:T(8,128)(2,1)}, u32[]{:S(2)}) copy-start(bf16[256,128]{1,0:T(8,128)(2,1)} %constant.14.clone.left_ref) | copy-start | bytes 196612
  9.6 5.5 %copy-start.4 = (bf16[128,256]{1,0:T(8,128)(2,1)S(1)}, bf16[128,256]{1,0:T(8,128)(2,1)}, u32[]{:S(2)}) copy-start(bf16[128,256]{1,0:T(8,128)(2,1)} %constant.13.clone.first_ref) | copy-start | bytes 196612
  9.8 7.1 %collective-permute-start.2 = (bf16[16,1536]{1,0:T(8,128)(2,1)S(1)}, bf16[16,1536]{1,0:T(8,128)(2,1)S(1)}, u32[]{:S(2)}, u32[]{:S(2)}) collective-permute-start(bf16[16,1536]{1,0:T(8,128)(2,1)S(1)} %get-tuple-element.23), channel_id=1, source_target_pairs={{0,1},{1,2},{2,3},{4,5},{5,6},{6,7},{8,9},{9,10},{10,11},{12,13},{... | collective-permute-start | bytes 147464 | tf_op jit(solution)/shard_map/ppermute | solution.py:383
  12.9 4.8 %collective-permute-start.3 = (bf16[16,1536]{1,0:T(8,128)(2,1)S(1)}, bf16[16,1536]{1,0:T(8,128)(2,1)S(1)}, u32[]{:S(2)}, u32[]{:S(2)}) collective-permute-start(bf16[16,1536]{1,0:T(8,128)(2,1)S(1)} %get-tuple-element.24), channel_id=1, source_target_pairs={{1,0},{2,1},{3,2},{5,4},{6,5},{7,6},{9,8},{10,9},{11,10},{13,12},{... | collective-permute-start | bytes 147464 | tf_op jit(solution)/shard_map/ppermute | solution.py:383
  15.1 2.6 %copy-start.2 = (bf16[4,160,256]{2,1,0:T(8,128)(2,1)S(1)}, bf16[4,160,256]{2,1,0:T(8,128)(2,1)}, u32[]{:S(2)}) copy-start(bf16[4,160,256]{2,1,0:T(8,128)(2,1)} %constant.15.clone.first_ref) | copy-start | bytes 983044
  19.3 21.6 %copy-start = (f32[256,32]{1,0:T(8,128)S(1)}, f32[256,32]{1,0:T(8,128)}, u32[]{:S(2)}) copy-start(f32[256,32]{1,0:T(8,128)} %constant.17.clone.places_ref) | copy-start | bytes 98308
  19.3 21.6 %copy-start.1 = (f32[64,32]{1,0:T(8,128)S(1)}, f32[64,32]{1,0:T(8,128)}, u32[]{:S(2)}) copy-start(f32[64,32]{1,0:T(8,128)} %constant.16.clone.rows_ref) | copy-start | bytes 24580
